TPU v7x, 32 devices: a whole 2x2x4 slice. The times are simulated.
32 devices in a mesh: dp: 16 (over z, x, core), tensor: 2 (over y).
Axes of the slice: x: 2, y: 2, z: 4, core: 2. Of those that a mesh axis runs over, the one named last changes fastest.
Arguments:
- tokens: bfloat16 [32, 256, 768], P('dp', 'tensor'), may hold values from -6 to 6
- w_qkv: bfloat16 [3, 768, 768], P(None, 'dp', 'tensor'), may hold values from -0.21875 to 0.21875
- qv_bias: float32 [2, 768], replicated, may hold values from -3 to 3
- w_proj: bfloat16 [768, 768], P(('tensor', 'dp')), may hold values from -2.5 to 2.5
- proj_bias: float32 [768], replicated, may hold values from -3 to 3
- w_up: bfloat16 [768, 3072], P('dp', 'tensor'), may hold values from -0.21875 to 0.21875
- up_bias: float32 [3072], replicated, may hold values from -3 to 3
- w_down: bfloat16 [3072, 768], P(('tensor', 'dp')), may hold values from -0.15625 to 0.15625
- down_bias: float32 [768], replicated, may hold values from -3 to 3
- norm1_gain: float32 [768], replicated, may hold values from 0.1 to 1.9
- norm1_shift: float32 [768], replicated, may hold values from -2 to 2
- norm2_gain: float32 [768], replicated, may hold values from 0.1 to 1.9
- norm2_shift: float32 [768], replicated, may hold values from -2 to 2
- rel_rows: bfloat16 [31, 64], replicated, may hold values from -0.59765625 to 0.59765625
- rel_cols: bfloat16 [31, 64], replicated, may hold values from -0.59765625 to 0.59765625
- cotangent: bfloat16 [32, 256, 768], P('dp', 'tensor'), may hold values from -6 to 6
Outputs:
- block_out: bfloat16 [32, 256, 768], P('dp', 'tensor')
- grad_tokens: float32 [32, 256, 768], P('dp', 'tensor')
- grad_w_qkv: float32 [3, 768, 768], P(None, 'dp', 'tensor')
- grad_qv_bias: float32 [2, 768], replicated
- grad_w_proj: float32 [768, 768], P(('tensor', 'dp'))
- grad_proj_bias: float32 [768], replicated
- grad_w_up: float32 [768, 3072], P('dp', 'tensor')
- grad_up_bias: float32 [3072], replicated
- grad_w_down: float32 [3072, 768], P(('tensor', 'dp'))
- grad_down_bias: float32 [768], replicated
- grad_norm1_gain: float32 [768], replicated
- grad_norm1_shift: float32 [768], replicated
- grad_norm2_gain: float32 [768], replicated
- grad_norm2_shift: float32 [768], replicated
- grad_rel_rows: float32 [31, 64], replicated
- grad_rel_cols: float32 [31, 64], replicated
All inputs are finite; a program needn't handle non-finite values.
Results may differ from a plain program's by a relative error of at most 0.015.
Values may be sent and summed in bfloat16 or wider, within the bound.
A program may use at most 192 MiB of HBM per device.

v0:
```python
import jax
import jax.numpy as jnp
from jax import lax
from jax.sharding import PartitionSpec as P

D = 768
HD = 64
FF = 3072
GRID = 16
MICRO = 2
RELS = 31


eps_norm = 1e-06


def layer_norm(values, gain_vec, shift_vec):
    row_mean = jnp.mean(values, axis=-1, keepdims=True)
    centred = values - row_mean
    second_moment = jnp.mean(centred * centred, axis=-1, keepdims=True)
    return centred * lax.rsqrt(second_moment + eps_norm) * gain_vec + shift_vec


def gelu_exact(values):
    return jax.nn.gelu(values, approximate=False)


def offset_table():
    grid_idx = jnp.arange(GRID, dtype=jnp.int32)
    offsets = grid_idx[:, None] - grid_idx[None, :] + (GRID - 1)
    return offsets[:, :, None] == jnp.arange(RELS, dtype=jnp.int32)[None, None, :]


def add_tuples(first_tup, second_tup):
    return tuple((left_term + right_term for left_term, right_term in zip(first_tup, second_tup)))


def block_scores(query_blk, key_all, rows_blk, cols_full):
    grid_rows = query_blk.shape[0] // GRID
    head_count = query_blk.shape[1]
    scores = jnp.einsum(
        "qhc,khc->hqk", query_blk, key_all, preferred_element_type=jnp.float32
    ) * HD ** (-0.5)
    query_grid = query_blk.reshape(grid_rows, GRID, head_count, HD)
    along_rows = jnp.einsum(
        "awhc,akc->hawk", query_grid, rows_blk, preferred_element_type=jnp.float32
    )
    along_cols = jnp.einsum(
        "awhc,wkc->hawk", query_grid, cols_full, preferred_element_type=jnp.float32
    )
    scores = (
        scores.reshape(head_count, grid_rows, GRID, GRID, GRID)
        + along_rows[..., :, None]
        + along_cols[..., None, :]
    )
    return scores.reshape(head_count, grid_rows * GRID, GRID * GRID)


def attend(query_all, key_all, value_all, rows_full, cols_full):
    token_count = query_all.shape[0]
    head_count = query_all.shape[1]
    block_rows = min(512, token_count)
    block_count = token_count // block_rows

    def one_block(packed):
        query_blk, block_idx = packed
        scores = block_scores(query_blk, key_all, rows_full, cols_full)
        top_score = jnp.max(scores, axis=-1, keepdims=True)
        log_total = top_score + jnp.log(
            jnp.sum(jnp.exp(scores - top_score), axis=-1, keepdims=True)
        )
        probs = jnp.exp(scores - log_total).astype(jnp.bfloat16)
        mixed_blk = jnp.einsum("hqk,khc->qhc", probs, value_all, preferred_element_type=jnp.float32)
        return (mixed_blk.astype(jnp.bfloat16), log_total)

    blocks = query_all.reshape(block_count, block_rows, head_count, HD)
    mixed_out, log_total = lax.map(one_block, (blocks, jnp.arange(block_count, dtype=jnp.int32)))
    return (mixed_out.reshape(token_count, head_count * HD), log_total)


def attend_back(query_all, key_all, value_all, grad_mixed, log_total, rows_full, cols_full):
    token_count = query_all.shape[0]
    head_count = query_all.shape[1]
    block_rows = min(512, token_count)
    block_count = token_count // block_rows
    grid_rows = block_rows // GRID
    highest = lax.Precision.HIGHEST
    cols_wide = cols_full.astype(jnp.float32)
    att_scale = HD ** (-0.5)

    def one_block(carry, packed):
        grad_keys, grad_vals, grad_cols = carry
        query_blk, grad_blk, log_blk, block_idx = packed
        scores = block_scores(query_blk, key_all, rows_full, cols_full)
        probs = jnp.exp(scores - log_blk)
        grad_probs = jnp.einsum(
            "qhc,khc->hqk", grad_blk, value_all, preferred_element_type=jnp.float32
        )
        inner_sum = jnp.sum(grad_probs * probs, axis=-1, keepdims=True)
        grad_scores = (probs * (grad_probs - inner_sum)).astype(jnp.bfloat16)
        probs_low = probs.astype(jnp.bfloat16)
        grad_vals = grad_vals + jnp.einsum(
            "hqk,qhc->khc", probs_low, grad_blk, preferred_element_type=jnp.float32
        )
        grad_keys = grad_keys + att_scale * jnp.einsum(
            "hqk,qhc->khc", grad_scores, query_blk, preferred_element_type=jnp.float32
        )
        grad_query = att_scale * jnp.einsum(
            "hqk,khc->qhc", grad_scores, key_all, preferred_element_type=jnp.float32
        )
        grid_scores = grad_scores.reshape(head_count, grid_rows, GRID, GRID, GRID)
        row_grad = jnp.sum(grid_scores, axis=-1, dtype=jnp.float32)
        col_grad = jnp.sum(grid_scores, axis=-2, dtype=jnp.float32)
        query_grid = query_blk.reshape(grid_rows, GRID, head_count, HD).astype(jnp.float32)
        rows_wide = rows_full.astype(jnp.float32)
        rel_query = jnp.einsum(
            "hawk,akc->awhc", row_grad, rows_wide, precision=highest
        ) + jnp.einsum("hawk,wkc->awhc", col_grad, cols_wide, precision=highest)
        grad_query = grad_query + rel_query.reshape(block_rows, head_count, HD)
        grad_rows_blk = jnp.einsum("hawk,awhc->akc", row_grad, query_grid, precision=highest)
        grad_cols = grad_cols + jnp.einsum(
            "hawk,awhc->wkc", col_grad, query_grid, precision=highest
        )
        return ((grad_keys, grad_vals, grad_cols), (grad_query, grad_rows_blk))

    blocks = query_all.reshape(block_count, block_rows, head_count, HD)
    grad_blocks = grad_mixed.reshape(block_count, block_rows, head_count, HD)
    zero_keys = jnp.zeros((token_count, head_count, HD), jnp.float32)
    zero_cols = jnp.zeros((GRID, GRID, HD), jnp.float32)
    (grad_keys, grad_vals, grad_cols), (grad_query, grad_rows) = lax.scan(
        one_block,
        (zero_keys, zero_keys, zero_cols),
        (blocks, grad_blocks, log_total, jnp.arange(block_count, dtype=jnp.int32)),
    )
    return (
        grad_query.reshape(token_count, head_count, HD),
        grad_keys,
        grad_vals,
        grad_rows.reshape(GRID, GRID, HD),
        grad_cols,
    )


def on_device(
    tokens,
    w_qkv,
    qv_bias,
    w_proj,
    proj_bias,
    w_up,
    up_bias,
    w_down,
    down_bias,
    norm1_gain,
    norm1_shift,
    norm2_gain,
    norm2_shift,
    rel_rows,
    rel_cols,
    cotangent,
):
    highest = lax.Precision.HIGHEST
    tensor_pos = lax.axis_index("tensor")
    width_dev = w_qkv.shape[2]
    hidden_dev = w_up.shape[1]
    head_dev = width_dev // HD
    bias_pair = lax.dynamic_slice_in_dim(qv_bias, tensor_pos * width_dev, width_dev, 1)
    bias_qkv = jnp.stack([bias_pair[0], jnp.zeros_like(bias_pair[0]), bias_pair[1]])
    bias_up = lax.dynamic_slice_in_dim(up_bias, tensor_pos * hidden_dev, hidden_dev, 0)
    chooser = offset_table()
    chooser_low = chooser.astype(jnp.bfloat16)
    chooser_wide = chooser.astype(jnp.float32)
    rows_full = jnp.einsum(
        "abr,rc->abc", chooser_low, rel_rows, preferred_element_type=jnp.float32
    ).astype(jnp.bfloat16)
    cols_full = jnp.einsum(
        "abr,rc->abc", chooser_low, rel_cols, preferred_element_type=jnp.float32
    ).astype(jnp.bfloat16)

    def fetch_weights():
        return (
            lax.all_gather(w_qkv, "dp", axis=1, tiled=True),
            lax.all_gather(w_proj, "dp", axis=0, tiled=True),
            lax.all_gather(w_up, "dp", axis=0, tiled=True),
            lax.all_gather(w_down, "dp", axis=0, tiled=True),
        )

    def spread(values):
        return lax.all_gather(values, "tensor", axis=0, tiled=True)

    def collect(values):
        return lax.psum_scatter(
            values.astype(jnp.bfloat16), "tensor", scatter_dimension=0, tiled=True
        ).astype(jnp.float32)

    outputs_list = []
    grad_list = []
    small_total = None
    big_total = None
    shard_total = None
    for micro_idx in range(MICRO):
        fwd_weights = fetch_weights()
        forward_qkv_w, forward_proj_w, forward_up_w, forward_down_w = fwd_weights
        start_res = tokens[micro_idx].astype(jnp.float32)
        first_norm, forward_norm1_back = jax.vjp(layer_norm, start_res, norm1_gain, norm1_shift)
        forward_first_all = spread(first_norm.astype(jnp.bfloat16))
        forward_token_count = forward_first_all.shape[0]
        proj_qkv = (
            jnp.einsum(
                "td,sde->ste", forward_first_all, forward_qkv_w, preferred_element_type=jnp.float32
            )
            + bias_qkv[:, None, :]
        )
        forward_heads_view = proj_qkv.astype(jnp.bfloat16).reshape(
            3, forward_token_count, head_dev, HD
        )
        forward_mixed_out, forward_log_total = attend(
            forward_heads_view[0],
            forward_heads_view[1],
            forward_heads_view[2],
            rows_full,
            cols_full,
        )
        attn_part = collect(
            jnp.dot(forward_mixed_out, forward_proj_w, preferred_element_type=jnp.float32)
        )
        middle = start_res + attn_part + proj_bias
        second_norm, forward_norm2_back = jax.vjp(layer_norm, middle, norm2_gain, norm2_shift)
        forward_second_all = spread(second_norm.astype(jnp.bfloat16))
        pre_act = (
            jnp.dot(forward_second_all, forward_up_w, preferred_element_type=jnp.float32) + bias_up
        )
        activated, forward_gelu_back = jax.vjp(gelu_exact, pre_act)
        forward_activ_low = activated.astype(jnp.bfloat16)
        mlp_part = collect(
            jnp.dot(forward_activ_low, forward_down_w, preferred_element_type=jnp.float32)
        )
        result = (middle + mlp_part + down_bias).astype(jnp.bfloat16)
        forward_saved = (
            forward_norm1_back,
            forward_first_all,
            forward_heads_view,
            forward_mixed_out,
            forward_log_total,
            forward_norm2_back,
            forward_second_all,
            forward_gelu_back,
            forward_activ_low,
        )
        result, saved = (result, forward_saved)
        bwd_weights = fetch_weights()
        grad_out = cotangent[micro_idx]
        qkv_w, proj_w, up_w, down_w = bwd_weights
        (
            norm1_back,
            first_all,
            heads_view,
            mixed_out,
            log_total,
            norm2_back,
            second_all,
            gelu_back,
            activ_low,
        ) = saved
        token_count = first_all.shape[0]
        grad_top = grad_out.astype(jnp.float32)
        top_all = spread(grad_out)
        grad_down_w = jnp.einsum(
            "tf,td->fd", activ_low, top_all, preferred_element_type=jnp.float32
        )
        grad_activ = jnp.einsum("td,fd->tf", top_all, down_w, preferred_element_type=jnp.float32)
        grad_pre = gelu_back(grad_activ)[0].astype(jnp.bfloat16)
        grad_up_w = jnp.einsum(
            "td,tf->df", second_all, grad_pre, preferred_element_type=jnp.float32
        )
        grad_second = collect(
            jnp.einsum("tf,df->td", grad_pre, up_w, preferred_element_type=jnp.float32)
        )
        grad_mid_norm, grad_gain2, grad_shift2 = norm2_back(grad_second)
        grad_middle = grad_top + grad_mid_norm
        middle_all = spread(grad_middle.astype(jnp.bfloat16))
        grad_proj_w = jnp.einsum(
            "te,td->ed", mixed_out, middle_all, preferred_element_type=jnp.float32
        )
        grad_mixed = jnp.einsum(
            "td,ed->te", middle_all, proj_w, preferred_element_type=jnp.float32
        ).astype(jnp.bfloat16)
        grad_query, grad_keys, grad_vals, grad_rows_exp, grad_cols_exp = attend_back(
            heads_view[0],
            heads_view[1],
            heads_view[2],
            grad_mixed.reshape(token_count, head_dev, HD),
            log_total,
            rows_full,
            cols_full,
        )
        grad_qkv = (
            jnp.stack([grad_query, grad_keys, grad_vals])
            .reshape(3, token_count, width_dev)
            .astype(jnp.bfloat16)
        )
        grad_qkv_w = jnp.einsum(
            "td,ste->sde", first_all, grad_qkv, preferred_element_type=jnp.float32
        )
        grad_first = collect(
            jnp.einsum("ste,sde->td", grad_qkv, qkv_w, preferred_element_type=jnp.float32)
        )
        grad_norm_in, grad_gain1, grad_shift1 = norm1_back(grad_first)
        grad_start = grad_middle + grad_norm_in
        qkv_sums = jnp.sum(grad_qkv, axis=1, dtype=jnp.float32)
        grad_pair = lax.dynamic_update_slice_in_dim(
            jnp.zeros((2, D), jnp.float32),
            jnp.stack([qkv_sums[0], qkv_sums[2]]),
            tensor_pos * width_dev,
            1,
        )
        grad_up_full = lax.dynamic_update_slice_in_dim(
            jnp.zeros((FF,), jnp.float32),
            jnp.sum(grad_pre, axis=0, dtype=jnp.float32),
            tensor_pos * hidden_dev,
            0,
        )
        grad_rel_r = jnp.einsum("abr,abc->rc", chooser_wide, grad_rows_exp, precision=highest)
        grad_rel_c = jnp.einsum("abr,abc->rc", chooser_wide, grad_cols_exp, precision=highest)
        small_terms = (
            grad_gain1,
            grad_shift1,
            grad_gain2,
            grad_shift2,
            grad_pair,
            jnp.sum(grad_middle, axis=0),
            grad_up_full,
            jnp.sum(grad_top, axis=0),
            grad_rel_r,
            grad_rel_c,
        )
        big_terms = (grad_qkv_w, grad_proj_w, grad_up_w, grad_down_w)
        grad_start, big_terms, small_terms = (grad_start, big_terms, small_terms)
        outputs_list.append(result)
        grad_list.append(grad_start)
        small_total = small_terms if micro_idx == 0 else add_tuples(small_total, small_terms)
        big_total = big_terms if micro_idx == 0 else add_tuples(big_total, big_terms)
    shard_total = (
        lax.psum_scatter(big_total[0], "dp", scatter_dimension=1, tiled=True),
        lax.psum_scatter(big_total[1], "dp", scatter_dimension=0, tiled=True),
        lax.psum_scatter(big_total[2], "dp", scatter_dimension=0, tiled=True),
        lax.psum_scatter(big_total[3], "dp", scatter_dimension=0, tiled=True),
    )
    small_sums = lax.psum(
        (
            small_total[0],
            small_total[1],
            small_total[2],
            small_total[3],
            small_total[4],
            small_total[5],
            small_total[6],
            small_total[7],
            small_total[8],
            small_total[9],
        ),
        ("dp", "tensor"),
    )
    block_out = jnp.stack(outputs_list)
    grad_tokens = jnp.stack(grad_list)
    return (
        block_out,
        grad_tokens,
        shard_total[0],
        small_sums[4],
        shard_total[1],
        small_sums[5],
        shard_total[2],
        small_sums[6],
        shard_total[3],
        small_sums[7],
        small_sums[0],
        small_sums[1],
        small_sums[2],
        small_sums[3],
        small_sums[8],
        small_sums[9],
    )


def solution(mesh):
    return jax.shard_map(
        on_device,
        mesh=mesh,
        in_specs=(
            P("dp", "tensor", None),
            P(None, "dp", "tensor"),
            P(),
            P(("tensor", "dp"), None),
            P(),
            P("dp", "tensor"),
            P(),
            P(("tensor", "dp"), None),
            P(),
            P(),
            P(),
            P(),
            P(),
            P(),
            P(),
            P("dp", "tensor", None),
        ),
        out_specs=(
            P("dp", "tensor", None),
            P("dp", "tensor", None),
            P(None, "dp", "tensor"),
            P(),
            P(("tensor", "dp"), None),
            P(),
            P("dp", "tensor"),
            P(),
            P(("tensor", "dp"), None),
            P(),
            P(),
            P(),
            P(),
            P(),
            P(),
            P(),
        ),
        check_vma=False,
    )
```

profile of v0, /device:TPU:0, one launch (start us, length us, event | category | flops | bytes accessed | tf_op | source)
XLA Modules:
  0.0 799.5 jit_solution(9421066556194583908)
XLA Ops:
  12.6 8.5 %all_gather.48 = bf16[256,768]{1,0:T(8,128)(2,1)S(1)} all-gather(bf16[128,768]{1,0:T(8,128)(2,1)S(1)} %fusion.60), channel_id=1, replica_groups=mesh['dp'=16,'tensor'=2] {'tensor'}, dimensions={0}, use_global_device_ids=true | all-gather | bytes 589824 | tf_op jit(solution)/shard_map/all_gather | solution.py:189
  22.2 24.2 %all_gather.50 = bf16[384,768]{1,0:T(8,128)(2,1)S(1)} all-gather(bf16[24,768]{1,0:T(8,128)(2,1)S(1)} %copy-done.88), channel_id=1, replica_groups=mesh['dp'=16,'tensor'=2] {'dp'}, dimensions={0}, use_global_device_ids=true | all-gather | bytes 626688 | tf_op jit(solution)/shard_map/all_gather | solution.py:183
  46.4 7.9 all-gather.6.cloned.1.call-done
  65.9 9.7 %add.426 = f32[6,256,256]{1,2,0:T(8,128)} reshape(f32[6,16,16,16,16]{2,1,4,3,0:T(8,128)} %add.425) | data formatting | bytes 3145728 | tf_op jit(solution)/shard_map/while/body/eval_jaxpr/add | solution.py:52
  81.7 9.7 %add.429 = f32[6,256,256]{1,2,0:T(8,128)} reshape(f32[6,16,16,16,16]{2,1,4,3,0:T(8,128)} %add.428) | data formatting | bytes 3145728 | tf_op jit(solution)/shard_map/while/body/eval_jaxpr/add | solution.py:52
  96.3 12.1 %reduce-scatter.12.cloned.1.call-done = bf16[128,768]{1,0:T(8,128)(2,1)} async-done(((bf16[256,768]{1,0:T(8,128)(2,1)}), bf16[128,768]{1,0:T(8,128)(2,1)}) %reduce-scatter.12.cloned.1.call-update) | async-done | bytes 196624 | tf_op jit(solution)/shard_map/reduce_scatter | solution.py:192
  110.3 7.5 all_gather.54
  135.5 9.7 %add.448 = f32[6,256,256]{1,2,0:T(8,128)} reshape(f32[6,16,16,16,16]{2,1,4,3,0:T(8,128)} %add.447) | data formatting | bytes 3145728 | tf_op jit(solution)/shard_map/while/body/eval_jaxpr/add | solution.py:52
  151.3 9.7 %add.451 = f32[6,256,256]{1,2,0:T(8,128)} reshape(f32[6,16,16,16,16]{2,1,4,3,0:T(8,128)} %add.450) | data formatting | bytes 3145728 | tf_op jit(solution)/shard_map/while/body/eval_jaxpr/add | solution.py:52
  170.4 11.4 %all-gather.1 = bf16[1,256,768]{2,1,0:T(8,128)(2,1)} all-gather(bf16[1,128,768]{2,1,0:T(8,128)(2,1)S(1)} %get-tuple-element.260), channel_id=3, replica_groups=mesh['dp'=16,'tensor'=2] {'tensor'}, dimensions={1}, use_global_device_ids=true | all-gather | bytes 589824 | tf_op jit(solution)/shard_map/all_gather | solution.py:189
  193.2 8.1 %all_gather.51 = bf16[256,768]{1,0:T(8,128)(2,1)} all-gather(bf16[128,768]{1,0:T(8,128)(2,1)S(1)} %get-tuple-element.256), channel_id=1, replica_groups=mesh['dp'=16,'tensor'=2] {'tensor'}, dimensions={0}, use_global_device_ids=true | all-gather | bytes 589824 | tf_op jit(solution)/shard_map/all_gather | solution.py:189
  208.1 19.1 %all-gather.8.cloned.1.call-done = bf16[768,1536]{1,0:T(8,128)(2,1)} async-done(((bf16[48,1536]{1,0:T(8,128)(2,1)}), bf16[768,1536]{1,0:T(8,128)(2,1)}) %all-gather.8.cloned.1.call-update) | async-done | bytes 2359312 | tf_op jit(solution)/shard_map/all_gather | solution.py:184
  227.3 7.5 multiply_convert_fusion.2
  234.8 35.7 %all-gather.10.cloned.1.call-done = bf16[1536,768]{1,0:T(8,128)(2,1)} async-done(((bf16[96,768]{1,0:T(8,128)(2,1)}), bf16[1536,768]{1,0:T(8,128)(2,1)}) %all-gather.10.cloned.1.call-update) | async-done | bytes 2359312 | tf_op jit(solution)/shard_map/all_gather | solution.py:185
  295.9 9.8 %reduce-scatter.20.cloned.1.call-done = bf16[128,768]{1,0:T(8,128)(2,1)} async-done(((bf16[256,768]{1,0:T(8,128)(2,1)}), bf16[128,768]{1,0:T(8,128)(2,1)}) %reduce-scatter.20.cloned.1.call-update) | async-done | bytes 196624 | tf_op jit(solution)/shard_map/reduce_scatter | solution.py:192
  305.8 15.4 %reduce-scatter.14.cloned.1.call-done = bf16[128,768]{1,0:T(8,128)(2,1)} async-done(((bf16[256,768]{1,0:T(8,128)(2,1)}), bf16[128,768]{1,0:T(8,128)(2,1)}) %reduce-scatter.14.cloned.1.call-update) | async-done | bytes 196624 | tf_op jit(solution)/shard_map/reduce_scatter | solution.py:192
  325.1 11.5 %reduce-scatter.18.cloned.1.call-done = bf16[128,768]{1,0:T(8,128)(2,1)} async-done(((bf16[256,768]{1,0:T(8,128)(2,1)}), bf16[128,768]{1,0:T(8,128)(2,1)}) %reduce-scatter.18.cloned.1.call-update) | async-done | bytes 196624 | tf_op jit(solution)/shard_map/reduce_scatter | solution.py:192
  372.2 8.0 %reshape.309 = f32[6,16,16,16,16]{2,1,4,3,0:T(8,128)} reshape(bf16[6,256,256]{1,2,0:T(8,128)(2,1)} %copy-done.7) | data formatting | bytes 2359296 | tf_op jit(solution)/shard_map/while/body/eval_jaxpr/convert_element_type | solution.py:113
  392.3 11.0 %fusion.128 = (f32[6,16,16,16]{2,1,3,0:T(8,128)S(1)}, f32[6,16,16,16]{2,1,3,0:T(8,128)}, f32[6,16,16,16]{2,1,3,0:T(8,128)}, f32[6,16,16,16]{2,1,3,0:T(8,128)S(1)}) fusion(f32[6,16,16,16,16]{2,1,4,3,0:T(8,128)} %reshape.309, f32[6,16,16,16,16]{2,1,4,3,0:T(8,128)} %reshape.310), kind=kLoop, calls=%fused_computation.260 | loop fusion | flops 1474560 | bytes 3538944 | tf_op jit(solution)/shard_map/while/body/eval_jaxpr/reduce_sum | solution.py:112
  471.4 42.5 %all-reduce.1 = (f32[2,768]{1,0:T(2,128)}, f32[768]{0:T(1024)}, f32[3072]{0:T(1024)}, f32[768]{0:T(1024)}, f32[768]{0:T(1024)}, /*index=5*/f32[768]{0:T(1024)}, ...) all-reduce(f32[2,768]{1,0:T(2,128)S(1)} %fusion.121, ...), channel_id=1, replica_groups=mesh['dp'=16,'tensor'=2] {'dp','tensor'}, use_global_device_ids=true, to_apply=%region_37.38 | all-reduce | flops 13184 | bytes 105472 | tf_op jit(solution)/shard_map/psum | solution.py:349
  515.2 57.1 %all-reduce.4.cloned.1.call-done = f32[3,768,384]{2,0,1:T(4,128)} async-done(((f32[3,768,384]{2,0,1:T(4,128)}), f32[3,768,384]{2,0,1:T(4,128)}) %all-reduce.4.cloned.1.call-update) | async-done | bytes 3538960
  574.0 60.3 %reduce-scatter.28.cloned.1.call-done = f32[24,768]{1,0:T(8,128)} async-done(((f32[384,768]{1,0:T(8,128)}), f32[24,768]{1,0:T(8,128)}) %reduce-scatter.28.cloned.1.call-update) | async-done | bytes 73744 | tf_op jit(solution)/shard_map/reduce_scatter | solution.py:345
  634.3 78.9 %reduce-scatter.32.cloned.1.call-done = f32[96,768]{1,0:T(8,128)} async-done(((f32[1536,768]{1,0:T(8,128)}), f32[96,768]{1,0:T(8,128)}) %reduce-scatter.32.cloned.1.call-update) | async-done | bytes 294928 | tf_op jit(solution)/shard_map/reduce_scatter | solution.py:347
  713.2 79.4 %reduce-scatter.30.cloned.1.call-done = f32[48,1536]{1,0:T(8,128)} async-done(((f32[768,1536]{1,0:T(8,128)}), f32[48,1536]{1,0:T(8,128)}) %reduce-scatter.30.cloned.1.call-update) | async-done | bytes 294928 | tf_op jit(solution)/shard_map/reduce_scatter | solution.py:346
  (463 shorter events, 227.9 us)
Async XLA Ops:
  7.2 47.1 %all-gather.6.cloned.1.call-start = ((), (), s32[]{:S(2)}) async-start(), calls=%async_computation.11 | async-start | bytes 1880064 | tf_op jit(solution)/shard_map/all_gather | solution.py:182
  8.0 100.5 %reduce-scatter.12.cloned.1.call-start = ((), (), s32[]{:S(2)}) async-start(), calls=%async_computation.12 | async-start | bytes 589824 | tf_op jit(solution)/shard_map/reduce_scatter | solution.py:192
  21.5 37.4 %copy-start.64 = (bf16[16,16,64,1]{2,1,3,0:T(8,128)(2,1)}, bf16[16,16,64,1]{2,1,3,0:T(8,128)(2,1)S(1)}, u32[]{:S(2)}) copy-start(bf16[16,16,64,1]{2,1,3,0:T(8,128)(2,1)S(1)} %fusion.30) | copy-start | bytes 98308
  22.2 35.2 %copy-start.67 = (bf16[16,16,64]{2,1,0:T(8,128)(2,1)}, bf16[16,16,64]{2,1,0:T(8,128)(2,1)S(1)}, u32[]{:S(2)}) copy-start(bf16[16,16,64]{2,1,0:T(8,128)(2,1)S(1)} %convolution_convert_fusion.12) | copy-start | bytes 98308
  46.4 48.0 %copy-start.3 = (bf16[384,768]{1,0:T(8,128)(2,1)}, bf16[384,768]{1,0:T(8,128)(2,1)S(1)}, u32[]{:S(2)}) copy-start(bf16[384,768]{1,0:T(8,128)(2,1)S(1)} %all_gather.50) | copy-start | bytes 1769476
  57.4 36.6 %copy-start.48 = (bf16[1,256,384]{1,2,0:T(8,128)(2,1)}, bf16[1,256,384]{1,2,0:T(8,128)(2,1)S(1)}, u32[]{:S(2)}) copy-start(bf16[1,256,384]{1,2,0:T(8,128)(2,1)S(1)} %copy.116) | copy-start | bytes 589828
  96.3 92.5 %reduce-scatter.16.cloned.1.call-start = ((), (), s32[]{:S(2)}) async-start(), calls=%async_computation.16 | async-start | bytes 589824 | tf_op jit(solution)/shard_map/reduce_scatter | solution.py:192
  166.7 60.5 %all-gather.8.cloned.1.call-start = ((), (), s32[]{:S(2)}) async-start(), calls=%async_computation.13 | async-start | bytes 2506752 | tf_op jit(solution)/shard_map/all_gather | solution.py:184
  167.3 103.2 %all-gather.10.cloned.1.call-start = ((), (), s32[]{:S(2)}) async-start(), calls=%async_computation.14 | async-start | bytes 2506752 | tf_op jit(solution)/shard_map/all_gather | solution.py:185
  167.9 128.0 %reduce-scatter.24.cloned.1.call-start = ((), (), s32[]{:S(2)}) async-start(), calls=%async_computation.20 | async-start | bytes 589824 | tf_op jit(solution)/shard_map/reduce_scatter | solution.py:192
  277.6 28.1 %reduce-scatter.20.cloned.1.call-start = ((), (), s32[]{:S(2)}) async-start(), calls=%async_computation.18 | async-start | bytes 589824 | tf_op jit(solution)/shard_map/reduce_scatter | solution.py:192
  288.6 32.5 %reduce-scatter.14.cloned.1.call-start = ((), (), s32[]{:S(2)}) async-start(), calls=%async_computation.15 | async-start | bytes 589824 | tf_op jit(solution)/shard_map/reduce_scatter | solution.py:192
  292.2 44.5 %reduce-scatter.18.cloned.1.call-start = ((), (), s32[]{:S(2)}) async-start(), calls=%async_computation.17 | async-start | bytes 589824 | tf_op jit(solution)/shard_map/reduce_scatter | solution.py:192
  295.7 172.5 %reduce-scatter.22.cloned.1.call-start = ((), (), s32[]{:S(2)}) async-start(), calls=%async_computation.19 | async-start | bytes 589824 | tf_op jit(solution)/shard_map/reduce_scatter | solution.py:192
  422.6 45.7 %reduce-scatter.26.cloned.1.call-start = ((), (), s32[]{:S(2)}) async-start(), calls=%async_computation.21 | async-start | bytes 589824 | tf_op jit(solution)/shard_map/reduce_scatter | solution.py:192
  430.9 141.4 %all-reduce.4.cloned.1.call-start = ((), (), s32[]{:S(2)}) async-start(), calls=%async_computation.25 | async-start | bytes 9437184
  441.5 192.8 %reduce-scatter.28.cloned.1.call-start = ((), (), s32[]{:S(2)}) async-start(), calls=%async_computation.22 | async-start | bytes 1253376 | tf_op jit(solution)/shard_map/reduce_scatter | solution.py:345
  444.8 268.3 %reduce-scatter.32.cloned.1.call-start = ((), (), s32[]{:S(2)}) async-start(), calls=%async_computation.24 | async-start | bytes 5013504 | tf_op jit(solution)/shard_map/reduce_scatter | solution.py:347
  449.2 343.3 %reduce-scatter.30.cloned.1.call-start = ((), (), s32[]{:S(2)}) async-start(), calls=%async_computation.23 | async-start | bytes 5013504 | tf_op jit(solution)/shard_map/reduce_scatter | solution.py:346
  466.7 47.3 %copy-start.18 = (f32[128,768]{1,0:T(8,128)S(1)}, f32[128,768]{1,0:T(8,128)}, u32[]{:S(2)}) copy-start(f32[128,768]{1,0:T(8,128)} %get-tuple-element.241) | copy-start | bytes 1179652
  466.7 47.3 %copy-start.20 = (f32[128,768]{1,0:T(8,128)S(1)}, f32[128,768]{1,0:T(8,128)}, u32[]{:S(2)}) copy-start(f32[128,768]{1,0:T(8,128)} %copy-done.19) | copy-start | bytes 1179652
  468.2 45.7 %copy-start.42 = (bf16[128,768]{1,0:T(8,128)(2,1)S(1)}, bf16[128,768]{1,0:T(8,128)(2,1)}, u32[]{:S(2)}) copy-start(bf16[128,768]{1,0:T(8,128)(2,1)} %reduce-scatter.22.cloned.1.call-done) | copy-start | bytes 589828
  468.3 45.6 %copy-start.43 = (bf16[128,768]{1,0:T(8,128)(2,1)S(1)}, bf16[128,768]{1,0:T(8,128)(2,1)}, u32[]{:S(2)}) copy-start(bf16[128,768]{1,0:T(8,128)(2,1)} %reduce-scatter.26.cloned.1.call-done) | copy-start | bytes 589828
  513.9 278.6 %copy-start.1 = (bf16[31,64]{1,0:T(8,128)(2,1)S(1)}, bf16[31,64]{1,0:T(8,128)(2,1)}, u32[]{:S(2)}) copy-start(bf16[31,64]{1,0:T(8,128)(2,1)} %param.29) | copy-start | bytes 11908
  (127 other events, 669.4 us)
Sparse Core Ops, SparseCore 0:
  10.4 43.9 all-gather.5
  96.4 12.0 reduce-scatter.11
  166.9 16.0 reduce-scatter.15
  185.1 42.0 all-gather.7
  229.4 41.0 all-gather.9
  277.8 11.8 reduce-scatter.23
  292.6 13.1 reduce-scatter.19
  308.0 13.0 reduce-scatter.13
  323.5 13.1 reduce-scatter.17
  422.7 13.1 reduce-scatter.21
  438.2 13.1 reduce-scatter.25
  454.9 117.3 all-reduce.3
  576.5 57.7 reduce-scatter.27
  638.6 74.5 reduce-scatter.31
  718.0 74.5 reduce-scatter.29
where the time goes:
time: 809 us; the launch traced here: 800 us
  waiting for transfers between devices  389 us (48%)
  blocking collectives  129 us (16%)
  local copies, waits for them, and re-layouts  126 us (16%)
  matrix products  94.7 us (12%)
  other arithmetic  42.4 us (5%)
  between operations  16.7 us (2%)
    reduce_scatter x1, waiting for transfers between devices, on_device(): lax.psum_scatter(big_total[2], 'dp', scatter_dimension=0, tiled=True)  79.4 us
    reduce_scatter x1, waiting for transfers between devices, on_device(): lax.psum_scatter(big_total[3], 'dp', scatter_dimension=0, tiled=True)  78.9 us
    all_gather x8, blocking collectives, spread(): return lax.all_gather(values, 'tensor', axis=0, tiled=True)  62.7 us
    add x8, local copies, waits for them, and re-layouts, block_scores(): scores.reshape(head_count, grid_rows, GRID, GRID, GRID)  62 us
    reduce_scatter x1, waiting for transfers between devices, on_device(): lax.psum_scatter(big_total[1], 'dp', scatter_dimension=0, tiled=True)  60.3 us
    unnamed x16, waiting for transfers between devices  59 us
    reduce_scatter x8, waiting for transfers between devices, collect(): lax.psum_scatter(values.astype(jnp.bfloat16), 'tensor', scatter_dimension...  48.9 us
    psum x1, blocking collectives, on_device(): lax.psum((small_total[0], small_total[1], small_total[2], small_total[3],...  42.5 us
  transfers between devices with their start and end apart: 15, of which 11 were waited for; matrix products, arithmetic and copies ran while one was open for 11% of the time, Pallas kernels for 0%

commit v1 on v0

v1 whole, which is shorter than its diff:
```python
import functools

import jax
import jax.numpy as jnp
from jax import lax
from jax.experimental import pallas as pl
from jax.experimental.pallas import tpu as pltpu
from jax.sharding import PartitionSpec as P

D = 768
HD = 64
FF = 3072
GRID = 16
TOK = 256
RELS = 31
NZ, NX, NC = 4, 2, 2
RING = NZ * NX * NC
IMG = 2
PAIR = 2 * HD
CH = 64
EPS = 1e-06
F32 = jnp.float32
BF = jnp.bfloat16
MESH = pl.DeviceIdType.MESH
SCALE = HD ** (-0.5)
QKV_M, PROJ_M, UP_M, DOWN_M = range(4)


def nn(a, b):
    return lax.dot_general(a, b, (((1,), (0,)), ((), ())), preferred_element_type=F32)


def nt(a, b):
    return lax.dot_general(a, b, (((1,), (1,)), ((), ())), preferred_element_type=F32)


def tn(a, b):
    return lax.dot_general(a, b, (((0,), (0,)), ((), ())), preferred_element_type=F32)


def iota(shape, dim):
    return lax.broadcasted_iota(jnp.int32, shape, dim)


def one_hot(cond):
    return jnp.where(cond, 1.0, 0.0).astype(BF)


def mean_last(v):
    return jnp.sum(v, axis=-1, keepdims=True) * (1.0 / v.shape[-1])


def normalize(v):
    centred = v - mean_last(v)
    rstd = lax.rsqrt(mean_last(centred * centred) + EPS)
    return centred * rstd, rstd


def norm_back(grad, n, rstd, gain):
    e = grad * gain
    return (e - mean_last(e) - n * mean_last(e * n)) * rstd


def spread_rows(v):
    return jnp.concatenate(
        [pltpu.roll(v[g * GRID : (g + 1) * GRID], g, 1) if g else v[:GRID] for g in range(GRID)], axis=0
    )


def spread_cols(v):
    return jnp.concatenate(
        [
            pltpu.roll(v[g * GRID : (g + 1) * GRID], 0, 1, stride=1, stride_axis=0)
            for g in range(GRID)
        ],
        axis=0,
    )


NAMES_IN = (
    "tok", "cot", "sq", "sp", "su", "sd",
    "qvb", "pjb", "upb", "dnb", "g1", "b1",
    "g2", "b2", "relr", "relc",
)
NAMES_OUT = (
    "o_blk", "o_gtok", "o_gq", "o_gp", "o_gu", "o_gd",
    "o_sm", "o_rel",
)


def scratch_table(width, hid):
    pairs = width // PAIR
    half = TOK // 2
    shards = [(3, D // RING, width), (width // RING, D), (D // RING, hid), (hid // RING, D)]
    table = {
        "XT": ((IMG, TOK, D), BF),
        "CT": ((IMG, TOK, D), BF),
        "WPB": ((width, D), BF),
        "FL": ((IMG, TOK, D), BF),
        "QKV": ((3, pairs, IMG, TOK, PAIR), BF),
        "PT": ((pairs, IMG, 2, TOK, TOK), BF),
        "MX": ((IMG, TOK, width), BF),
        "AP": ((IMG, TOK, D), BF),
        "APR": ((IMG, TOK, D), BF),
        "MID": ((IMG, TOK, D), F32),
        "N2": ((IMG, TOK, D), F32),
        "RS2": ((IMG, TOK, 128), F32),
        "SEC": ((IMG, TOK, D), BF),
        "ACT": ((IMG, TOK, hid), BF),
        "GEL": ((IMG, TOK, hid), BF),
        "DP": ((IMG, TOK, D), BF),
        "DPR": ((IMG, half, D), BF),
        "GPRE": ((IMG, TOK, hid), BF),
        "GS": ((IMG, TOK, D), BF),
        "GSR": ((IMG, TOK, D), BF),
        "GM": ((IMG, half, D), F32),
        "MIDL": ((IMG, TOK, D), BF),
        "GMX": ((IMG, TOK, width), BF),
        "GQKV": ((3, IMG, TOK, width), BF),
        "GF": ((IMG, TOK, D), BF),
        "GFR": ((IMG, half, D), BF),
        "RG": ((PAIR, PAIR), F32),
        "TBF": ((PAIR, PAIR), BF),
        "TBB": ((PAIR, PAIR), BF),
        "OHF": ((TOK, PAIR), BF),
        "OHB": ((TOK, PAIR), BF),
        "MSK": ((4, 16, PAIR), BF),
        "SMS": ((6, 16, D), F32),
        "SMR": ((5, 16, D), F32),
        "SRS": ((6, 64, 128), F32),
        "SRR": ((5, 64, 128), F32),
    }
    for i, shard in enumerate(shards):
        table[f"W{i}"] = ((NZ, NX, NC) + shard, BF)
        table[f"G{i}"] = ((NZ, NX, NC) + shard, BF)
        table[f"C{i}"] = ((NZ, NX) + shard, BF)
        table[f"X{i}"] = ((NZ,) + shard, BF)
        table[f"Z{i}"] = ((NZ - 1,) + shard, BF)
    sems = {
        "agz": (4, 3),
        "agx": (4, 4),
        "agc": (4, 8),
        "ysem": (10,),
        "rsc": (4,),
        "rsx": (4, 4),
        "rsz": (4, 3),
        "ars": (5, 2),
    }
    return table, sems, shards


class Refs:
    pass


def block_kernel(ratio, width, hid, names, *refs):
    k = Refs()
    for name, ref in zip(names, refs):
        setattr(k, name, ref)
    pairs = width // PAIR
    half = TOK // 2
    dp = lax.axis_index("dp")
    t = lax.axis_index("tensor")
    sub = lax.rem(dp, ratio)
    s = dp // ratio
    z, x, c = s // (NX * NC), lax.rem(s // NC, NX), lax.rem(s, NC)

    def device(zz, xx, cc, tt=t):
        return (((zz * NX + xx) * NC + cc) * ratio + sub, tt)

    def zrot(step):
        return lax.rem(z + step, NZ)

    core_peer, x_peer, y_peer = device(z, x, 1 - c), device(z, 1 - x, c), device(z, x, c, 1 - t)
    z_near = z + 1 - 2 * lax.rem(z, 2)
    z_far = lax.rem(z + 2, NZ)
    own0 = pl.multiple_of(t * half, half)
    other0 = pl.multiple_of((1 - t) * half, half)

    def remote(src, dst, sems, idx, peer):
        return pltpu.make_async_remote_copy(
            src_ref=src,
            dst_ref=dst,
            send_sem=getattr(k, sems + "_s").at[idx],
            recv_sem=getattr(k, sems + "_r").at[idx],
            device_id=peer,
            device_id_type=MESH,
        )

    shard_in = [k.sq, k.sp, k.su, k.sd]
    W = [k.W0, k.W1, k.W2, k.W3]
    G = [k.G0, k.G1, k.G2, k.G3]
    C = [k.C0, k.C1, k.C2, k.C3]
    X = [k.X0, k.X1, k.X2, k.X3]
    Z = [k.Z0, k.Z1, k.Z2, k.Z3]

    def ag_z(m, i):
        return remote(shard_in[m], W[m].at[z, x, c], "agz", (m, i - 1), device(zrot(i), x, c))

    def ag_x(m, i):
        zz = zrot(NZ - i)
        src = shard_in[m] if i == 0 else W[m].at[zz, x, c]
        return remote(src, W[m].at[zz, x, c], "agx", (m, i), x_peer)

    def ag_c(m, i, other):
        zz = zrot(NZ - i)
        xx = 1 - x if other else x
        src = shard_in[m] if i == 0 and not other else W[m].at[zz, xx, c]
        return remote(src, W[m].at[zz, xx, c], "agc", (m, i + 4 * other), core_peer)

    def ag_start(m):
        for i in (2, 1, 3):
            ag_z(m, i).start()
        ag_x(m, 0).start()
        ag_c(m, 0, 0).start()
        W[m][z, x, c] = shard_in[m][...]

    def ag_zdone(m):
        for i in (1, 3, 2):
            ag_z(m, i).wait_recv()
            ag_x(m, i).start()
            ag_c(m, i, 0).start()

    def ag_xdone(m):
        for i in (0, 1, 3, 2):
            ag_x(m, i).wait_recv()
            ag_c(m, i, 1).start()

    def ag_done(m):
        for other in (0, 1):
            for i in (0, 1, 3, 2):
                ag_c(m, i, other).wait_recv()

    def rs_core(m):
        return remote(G[m].at[:, :, 1 - c], C[m], "rsc", (m,), core_peer)

    def rs_x(m, zz):
        return remote(G[m].at[zz, 1 - x, c], X[m].at[zz], "rsx", (m, zz), x_peer)

    def rs_z(m, i):
        return remote(G[m].at[zrot(i), x, c], Z[m].at[i - 1], "rsz", (m, i - 1), device(zrot(i), x, c))

    def add_into(dst, where, src, which):
        if len(dst.shape) - len(where) == 3:
            for j in range(3):
                dst[(*where, j)] = dst[(*where, j)] + src[(*which, j)]
        else:
            dst[where] = dst[where] + src[which]

    def rs_core_done(m):
        rs_core(m).wait_recv()

        @pl.loop(0, NZ * NX)
        def _(i):
            zz, xx = i // NX, lax.rem(i, NX)
            add_into(G[m], (zz, xx, c), C[m], (zz, xx))

        for zz in range(NZ):
            rs_x(m, zz).start()

    def rs_x_done(m):
        for zz in range(NZ):
            rs_x(m, zz).wait_recv()

        @pl.loop(0, NZ)
        def _(zz):
            add_into(G[m], (zz, x, c), X[m], (zz,))

        for i in (2, 1, 3):
            rs_z(m, i).start()

    def rs_z_done(m, out):
        for i in (1, 2, 3):
            rs_z(m, i).wait_recv()
        parts = range(3) if m == QKV_M else (None,)
        for j in parts:
            at = () if j is None else (j,)
            total = G[m][(z, x, c, *at)].astype(F32)
            for i in range(3):
                total = total + Z[m][(i, *at)].astype(F32)
            if j is None:
                out[...] = total
            else:
                out[j] = total

    def y_rows(img, base):
        return (img, pl.ds(base, half))

    def y_tok():
        return remote(k.tok, k.XT.at[:, pl.ds(own0, half)], "ysem", (0,), y_peer)

    def y_cot():
        return remote(k.cot, k.CT.at[:, pl.ds(own0, half)], "ysem", (1,), y_peer)

    def y_attn(img):
        return remote(k.AP.at[img], k.APR.at[img], "ysem", (2 + img,), y_peer)

    def y_mlp(img):
        return remote(k.DP.at[img, pl.ds(other0, half)], k.DPR.at[img], "ysem", (4 + img,), y_peer)

    def y_sec(img):
        return remote(k.GS.at[img], k.GSR.at[img], "ysem", (6 + img,), y_peer)

    def y_first(img):
        return remote(k.GF.at[img, pl.ds(other0, half)], k.GFR.at[img], "ysem", (8 + img,), y_peer)

    def rows(base, i):
        return pl.ds(pl.multiple_of(base + i * CH, CH), CH)

    barrier = pltpu.get_barrier_semaphore()
    peers = [core_peer, x_peer, y_peer] + [device(zrot(i), x, c) for i in (1, 2, 3)]
    for peer in peers:
        pl.semaphore_signal(barrier, inc=1, device_id=peer, device_id_type=MESH)
    pl.semaphore_wait(barrier, len(peers))

    ag_start(QKV_M)
    y_tok().start()
    ag_start(PROJ_M)
    ag_start(UP_M)
    ag_start(DOWN_M)
    y_cot().start()

    lane = iota((TOK, PAIR), 1)
    lane64 = lax.rem(lane, HD)
    urow, ucol = iota((TOK, PAIR), 0) // GRID, lax.rem(iota((TOK, PAIR), 0), GRID)
    shifted = lax.rem(lane + (PAIR - GRID + 1), HD)
    seg, pos = shifted // GRID, lax.rem(shifted, GRID)
    k.OHF[...] = one_hot(((seg < 2) & (urow == pos)) | ((seg >= 2) & (ucol == pos)))
    k.OHB[...] = one_hot(
        ((lane64 < GRID) & (urow == GRID - 1 - lane64))
        | ((lane64 >= 2 * GRID) & (lane64 < 3 * GRID) & (ucol == 3 * GRID - 1 - lane64))
    )
    mlane = iota((16, PAIR), 1)
    in_first = mlane < HD
    ext_first = (mlane >= GRID - 1) & (mlane < HD + GRID - 1)
    k.MSK[0] = one_hot(in_first)
    k.MSK[1] = one_hot(mlane >= HD)
    k.MSK[2] = one_hot(ext_first)
    k.MSK[3] = one_hot((mlane < GRID - 1) | (mlane >= HD + GRID - 1))
    tl, td = iota((PAIR, RELS), 0), iota((PAIR, RELS), 1)
    fwd_tab = jnp.zeros((PAIR, PAIR), F32)
    bwd_tab = jnp.zeros((PAIR, PAIR), F32)
    for head in range(2):
        place = one_hot(iota((HD, PAIR), 1) == iota((HD, PAIR), 0) + head * HD)
        for base, rel in ((0, k.relr), (32, k.relc)):
            wide = nn(rel[...], place).astype(BF)
            at = tl - (head * HD + base)
            fwd_tab = fwd_tab + nn(one_hot(at == RELS - 1 - td), wide)
            bwd_tab = bwd_tab + nn(one_hot(at == td), wide)
    k.TBF[...] = fwd_tab.astype(BF)
    k.TBB[...] = bwd_tab.astype(BF)
    k.SMS[0] = jnp.zeros((16, D), F32)
    k.RG[...] = jnp.zeros((PAIR, PAIR), F32)

    def first_norm(base):
        @pl.loop(0, IMG)
        def _(img):
            @pl.loop(0, half // CH)
            def _(i):
                at = rows(base, i)
                n, _ = normalize(k.XT[img, at].astype(F32))
                k.FL[img, at] = (n * k.g1[...] + k.b1[...]).astype(BF)

    for img in range(IMG):
        k.XT[img, pl.ds(own0, half)] = k.tok[img]
        k.CT[img, pl.ds(own0, half)] = k.cot[img]
    first_norm(own0)
    ag_zdone(QKV_M)
    y_tok().wait_recv()
    first_norm(other0)
    ag_xdone(QKV_M)
    ag_zdone(PROJ_M)
    ag_done(QKV_M)

    lanes_w = pl.ds(pl.multiple_of(t * width, 128), width)
    for i in range(3):

        @pl.loop(0, IMG)
        def _(img):
            out = nn(k.FL[img], W[0][:, :, :, i].reshape(D, width))
            if i != 1:
                out = out + k.qvb[i // 2 : i // 2 + 1, lanes_w]
            low = out.astype(BF)
            for p in range(pairs):
                k.QKV[i, p, img] = low[:, p * PAIR : (p + 1) * PAIR]

    ag_zdone(UP_M)
    ag_xdone(PROJ_M)

    def head_mask(i):
        return k.MSK[i][0:1]

    def attend(step):
        img, p = step // pairs, lax.rem(step, pairs)
        q, key, val = k.QKV[0, p, img], k.QKV[1, p, img], k.QKV[2, p, img]
        qr = nt(q, k.TBF[...])
        ext = jnp.where(
            (lane64 >= 15) & (lane64 < 31),
            spread_rows(qr),
            jnp.where((lane64 >= 47) & (lane64 < 63), spread_cols(qr), 0.0),
        )
        high = ext.astype(BF).astype(F32)
        ext = (high + pltpu.roll(ext - high, GRID, 1)).astype(BF)
        k_ext = jnp.concatenate([key, k.OHF[...]], axis=1)
        probs, vals = [], []
        for head in range(2):
            q_ext = jnp.concatenate(
                [q * (head_mask(head) * SCALE).astype(BF), ext * head_mask(2 + head)], axis=1
            )
            scores = nt(k_ext, q_ext)
            e = jnp.exp(scores - jnp.max(scores, axis=0, keepdims=True))
            low = (e * (1.0 / jnp.sum(e, axis=0, keepdims=True))).astype(BF)
            k.PT[p, img, head] = low
            probs.append(low)
            vals.append(val * head_mask(head))
        mixed = tn(jnp.concatenate(probs, axis=0), jnp.concatenate(vals, axis=0))
        k.MX[img, :, pl.ds(pl.multiple_of(p * PAIR, PAIR), PAIR)] = mixed.astype(BF)

    def project(img):
        for j in range(D // 256):
            cols = slice(j * 256, (j + 1) * 256)
            k.AP[img, :, cols] = nn(k.MX[img], k.WPB[:, cols]).astype(BF)
        y_attn(img).start()

    @pl.loop(0, pairs)
    def _(step):
        attend(step)

    ag_xdone(UP_M)
    ag_zdone(DOWN_M)
    ag_done(PROJ_M)

    @pl.loop(0, RING)
    def _(i):
        zz, xx, cc = i // (NX * NC), lax.rem(i // NC, NX), lax.rem(i, NC)
        k.G1F[pl.ds(pl.multiple_of(i * (width // RING), 8), width // RING)] = W[1][zz, xx, cc].astype(F32)

    k.WPB[...] = k.G1F[...].astype(BF)
    project(0)

    @pl.loop(pairs, 2 * pairs)
    def _(step):
        attend(step)

    project(1)
    ag_xdone(DOWN_M)
    ag_done(UP_M)

    def second(img):
        y_attn(img).wait_recv()

        @pl.loop(0, TOK // CH)
        def _(i):
            at = rows(0, i)
            mid = (
                k.XT[img, at].astype(F32)
                + k.AP[img, at].astype(F32)
                + k.APR[img, at].astype(F32)
                + k.pjb[...]
            )
            k.MID[img, at] = mid
            n, rstd = normalize(mid)
            k.N2[img, at] = n
            k.RS2[img, at] = jnp.broadcast_to(rstd, (CH, 128))
            k.SEC[img, at] = (n * k.g2[...] + k.b2[...]).astype(BF)

        @pl.loop(0, hid // 256)
        def _(j):
            cols = pl.ds(pl.multiple_of(j * 256, 256), 256)
            bias = k.upb[0:1, pl.ds(pl.multiple_of(t * hid + j * 256, 256), 256)]
            pre = nn(k.SEC[img], W[2][:, :, :, :, cols].reshape(D, 256)) + bias
            phi = 0.5 + 0.5 * lax.erf(pre * 0.7071067811865476)
            k.ACT[img, :, cols] = (pre * phi).astype(BF)
            k.GEL[img, :, cols] = (phi + pre * (0.3989422804014327 * jnp.exp(-0.5 * pre * pre))).astype(BF)

    second(0)
    second(1)
    ag_done(DOWN_M)

    def down(img):
        @pl.loop(0, D // 256)
        def _(j):
            cols = pl.ds(pl.multiple_of(j * 256, 256), 256)
            k.DP[img, :, cols] = nn(k.ACT[img], W[3][:, :, :, :, cols].reshape(hid, 256)).astype(BF)

        y_mlp(img).start()

    y_cot().wait_recv()

    tile = hid // NZ

    @pl.loop(0, NZ)
    def _(m):
        lhs = k.ACT[:, :, pl.ds(pl.multiple_of(m * tile, 128), tile)].reshape(IMG * TOK, tile)
        for j in range(D // 256):
            cols = slice(j * 256, (j + 1) * 256)
            out = tn(lhs, k.CT[:, :, cols].reshape(IMG * TOK, 256)).astype(BF)
            G[3][m, :, :, :, cols] = out.reshape(NX, NC, hid // RING, 256)

    rs_core(DOWN_M).start()

    @pl.loop(0, NZ)
    def _(m):
        cols = pl.ds(pl.multiple_of(m * tile, 128), tile)
        sums = jnp.zeros((1, tile), F32)
        for img in range(IMG):
            grad = nt(k.CT[img], W[3][m].reshape(tile, D)) * k.GEL[img, :, cols].astype(F32)
            low = grad.astype(BF)
            k.GPRE[img, :, cols] = low
            sums = sums + jnp.sum(low.astype(F32), axis=0, keepdims=True)
        per_row = D // tile
        k.SMS[0, pl.ds(8 + t * (hid // D) + m // per_row, 1), pl.ds(pl.multiple_of(lax.rem(m, per_row) * tile, 128), tile)] = sums

    for img in range(IMG):

        @pl.loop(0, 2)
        def _(j):
            w = W[2][pl.ds(j * 2, 2)].reshape(D // 2, hid)
            k.GS[img, :, pl.ds(pl.multiple_of(j * (D // 2), 128), D // 2)] = nt(k.GPRE[img], w).astype(BF)

        y_sec(img).start()

    rs_core_done(DOWN_M)

    @pl.loop(0, hid // 256)
    def _(j):
        cols = pl.ds(pl.multiple_of(j * 256, 256), 256)
        rhs = k.GPRE[:, :, cols].reshape(IMG * TOK, 256)
        for m in range(2):
            lhs = k.SEC[:, :, m * (D // 2) : (m + 1) * (D // 2)].reshape(IMG * TOK, D // 2)
            out = tn(lhs, rhs).astype(BF)
            G[2][2 * m : 2 * m + 2, :, :, :, cols] = out.reshape(2, NX, NC, D // RING, 256)

    rs_core(UP_M).start()
    down(0)
    down(1)
    rs_core_done(UP_M)

    def middle_back(img, base, own):
        zero = jnp.zeros((1, D), F32)

        def chunk(i, sums):
            at = rows(base, i)
            grad = k.GS[img, at].astype(F32) + k.GSR[img, at].astype(F32)
            n = k.N2[img, at]
            rstd = jnp.concatenate([k.RS2[img, at]] * (D // 128), axis=1)
            cot = k.CT[img, at].astype(F32)
            gm = cot + norm_back(grad, n, rstd, k.g2[...])
            k.MIDL[img, at] = gm.astype(BF)
            if own:
                k.GM[img, rows(0, i)] = gm
                terms = (grad * n, grad, gm, cot)
                sums = tuple(a + jnp.sum(b, axis=0, keepdims=True) for a, b in zip(sums, terms))
            return sums

        return lax.fori_loop(0, half // CH, chunk, (zero,) * 4 if own else ())

    for img in range(IMG):
        y_sec(img).wait_recv()
        sums = middle_back(img, own0, True)
        for row, value in zip((2, 3, 6, 7), sums):
            k.SMS[0, row : row + 1] = k.SMS[0, row : row + 1] + value
        middle_back(img, other0, False)
        k.GMX[img] = nt(k.MIDL[img], k.WPB[...]).astype(BF)

    for j in range(D // 256):
        cols = slice(j * 256, (j + 1) * 256)
        out = tn(k.MX[...].reshape(IMG * TOK, width), k.MIDL[:, :, cols].reshape(IMG * TOK, 256))
        G[1][:, :, :, :, cols] = out.reshape(NZ, NX, NC, width // RING, 256).astype(BF)
    rs_core(PROJ_M).start()
    rs_x_done(DOWN_M)

    def attend_back(step):
        img, p = step // pairs, lax.rem(step, pairs)
        cols = pl.ds(pl.multiple_of(p * PAIR, PAIR), PAIR)
        q, key, val = k.QKV[0, p, img], k.QKV[1, p, img], k.QKV[2, p, img]
        gmx = k.GMX[img, :, cols]
        pts, gss, gms, qs, kes = [], [], [], [], []
        for head in range(2):
            m = head_mask(head)
            low = k.PT[p, img, head]
            probs = low.astype(F32)
            gp = nt(val * m, gmx)
            inner = jnp.sum(gp * probs, axis=0, keepdims=True)
            pts.append(low)
            gss.append((probs * (gp - inner)).astype(BF))
            gms.append(gmx * m)
            qs.append(q * (m * SCALE).astype(BF))
            kes.append(jnp.concatenate([key * (m * SCALE).astype(BF), k.OHB[...] * m], axis=1))
        grad_v = nn(jnp.concatenate(pts, axis=1), jnp.concatenate(gms, axis=0))
        grad_k = nn(jnp.concatenate(gss, axis=1), jnp.concatenate(qs, axis=0))
        both = tn(jnp.concatenate(gss, axis=0), jnp.concatenate(kes, axis=0))
        rel = both[:, PAIR:]
        rel = jnp.where(lane64 < 32, spread_rows(rel), spread_cols(rel))
        high = rel.astype(BF)
        rest = (rel - high.astype(F32)).astype(BF)
        grad_q = both[:, :PAIR] + nn(
            jnp.concatenate([high, rest], axis=1), jnp.concatenate([k.TBB[...]] * 2, axis=0)
        )
        k.RG[...] += tn(jnp.concatenate([high, rest], axis=0), jnp.concatenate([q, q], axis=0))
        lanes = pl.ds(pl.multiple_of(t * width + p * PAIR, PAIR), PAIR)
        for i, grad in enumerate((grad_q, grad_k, grad_v)):
            low = grad.astype(BF)
            k.GQKV[i, img, :, cols] = low
            if i != 1:
                row = 4 + i // 2
                k.SMS[0, row : row + 1, lanes] = k.SMS[0, row : row + 1, lanes] + jnp.sum(
                    low.astype(F32), axis=0, keepdims=True
                )

    @pl.loop(0, pairs)
    def _(step):
        attend_back(step)

    rs_core_done(PROJ_M)
    rs_x_done(UP_M)

    @pl.loop(pairs, 2 * pairs)
    def _(step):
        attend_back(step)

    for i in range(3):

        @pl.loop(0, 2)
        def _(m):
            lhs = k.FL[:, :, pl.ds(pl.multiple_of(m * (D // 2), 128), D // 2)].reshape(IMG * TOK, D // 2)
            out = tn(lhs, k.GQKV[i].reshape(IMG * TOK, width)).astype(BF)
            G[0][pl.ds(2 * m, 2), :, :, i] = out.reshape(2, NX, NC, D // RING, width)

    rs_core(QKV_M).start()

    for img in range(IMG):

        @pl.loop(0, 2)
        def _(m):
            total = jnp.zeros((TOK, D // 2), F32)
            for i in range(3):
                total = total + nt(k.GQKV[i, img], W[0][pl.ds(2 * m, 2), :, :, i].reshape(D // 2, width))
            k.GF[img, :, pl.ds(pl.multiple_of(m * (D // 2), 128), D // 2)] = total.astype(BF)

        y_first(img).start()

    rs_core_done(QKV_M)
    rs_x_done(PROJ_M)

    for img in range(IMG):
        y_mlp(img).wait_recv()
        y_first(img).wait_recv()

        def finish(i, sums):
            at, here = rows(own0, i), rows(0, i)
            k.o_blk[img, here] = (
                k.MID[img, at] + k.DP[img, at].astype(F32) + k.DPR[img, here].astype(F32) + k.dnb[...]
            ).astype(BF)
            n, rstd = normalize(k.tok[img, here].astype(F32))
            grad = k.GF[img, at].astype(F32) + k.GFR[img, here].astype(F32)
            k.o_gtok[img, here] = k.GM[img, here] + norm_back(grad, n, rstd, k.g1[...])
            terms = (grad * n, grad)
            return tuple(a + jnp.sum(b, axis=0, keepdims=True) for a, b in zip(sums, terms))

        sums = lax.fori_loop(0, half // CH, finish, (jnp.zeros((1, D), F32),) * 2)
        for row, value in enumerate(sums):
            k.SMS[0, row : row + 1] = k.SMS[0, row : row + 1] + value

    rg = k.RG[...]
    turned = pltpu.roll(rg, HD, 1)
    k.SRS[0, 0:32] = rg[0:32] + turned[64:96]
    k.SRS[0, 32:64] = rg[32:64] + turned[96:128]

    ar_peers = [core_peer, x_peer, y_peer, device(z_near, x, c), device(z_far, x, c)]

    def ar(i):
        return (
            remote(k.SMS.at[i], k.SMR.at[i], "ars", (i, 0), ar_peers[i]),
            remote(k.SRS.at[i], k.SRR.at[i], "ars", (i, 1), ar_peers[i]),
        )

    def ar_step(i):
        for copy in ar(i):
            copy.wait_recv()
        k.SMS[i + 1] = k.SMS[i] + k.SMR[i]
        k.SRS[i + 1] = k.SRS[i] + k.SRR[i]
        if i < 4:
            for copy in ar(i + 1):
                copy.start()

    for copy in ar(0):
        copy.start()
    ar_step(0)
    rs_x_done(QKV_M)
    rs_z_done(DOWN_M, k.o_gd)
    ar_step(1)
    rs_z_done(UP_M, k.o_gu)
    ar_step(2)
    rs_z_done(PROJ_M, k.o_gp)
    ar_step(3)
    ar_step(4)
    k.o_sm[...] = k.SMS[5]
    k.o_rel[...] = k.SRS[5]
    rs_z_done(QKV_M, k.o_gq)

    for m in range(4):
        for i in (1, 2, 3):
            ag_z(m, i).wait_send()
            rs_z(m, i).wait_send()
        for i in range(4):
            ag_x(m, i).wait_send()
            ag_c(m, i, 0).wait_send()
            ag_c(m, i, 1).wait_send()
            rs_x(m, i).wait_send()
        rs_core(m).wait_send()
    for copy in (y_tok(), y_cot()):
        copy.wait_send()
    for img in range(IMG):
        for make in (y_attn, y_mlp, y_sec, y_first):
            make(img).wait_send()
    for i in range(5):
        for copy in ar(i):
            copy.wait_send()


def fused_block(ratio, args):
    width, hid = args[2].shape[2], args[4].shape[1]
    table, sems, shards = scratch_table(width, hid)
    table["G1F"] = ((width, D), F32)
    names = list(NAMES_IN) + list(NAMES_OUT) + list(table)
    scratch = [pltpu.VMEM(shape, kind) for shape, kind in table.values()]
    for name, shape in sems.items():
        names += [name + "_s", name + "_r"]
        scratch += [pltpu.SemaphoreType.DMA(shape)] * 2
    tok = args[0].shape
    outs = [(tok, BF), (tok, F32)] + [(shape, F32) for shape in shards] + [((16, D), F32), ((64, 128), F32)]
    vmem = pl.BlockSpec(memory_space=pltpu.VMEM)
    return pl.pallas_call(
        functools.partial(block_kernel, ratio, width, hid, names),
        out_shape=[jax.ShapeDtypeStruct(shape, kind) for shape, kind in outs],
        in_specs=[vmem] * len(NAMES_IN),
        out_specs=[vmem] * len(outs),
        scratch_shapes=scratch,
        compiler_params=pltpu.CompilerParams(
            collective_id=0, has_side_effects=True, vmem_limit_bytes=62 << 20
        ),
        name="fused_block",
    )(*args)


def on_device(dp_size, *args):
    (tokens, w_qkv, qv_bias, w_proj, proj_bias, w_up, up_bias, w_down, down_bias,
     norm1_gain, norm1_shift, norm2_gain, norm2_shift, rel_rows, rel_cols, cotangent) = args
    ratio = dp_size // RING
    weights = [w_qkv, w_proj, w_up, w_down]
    dims = (1, 0, 0, 0)
    groups = [[i * ratio + j for j in range(ratio)] for i in range(RING)]
    across = [[i * ratio + j for i in range(RING)] for j in range(ratio)]
    if ratio > 1:
        weights = [
            lax.all_gather(w, "dp", axis=dim, tiled=True, axis_index_groups=groups)
            for w, dim in zip(weights, dims)
        ]
    flat = lambda v: v.reshape(1, -1)
    outs = fused_block(
        ratio,
        (tokens, cotangent, *weights, qv_bias, flat(proj_bias), flat(up_bias), flat(down_bias),
         flat(norm1_gain), flat(norm1_shift), flat(norm2_gain), flat(norm2_shift), rel_rows, rel_cols),
    )
    block_out, grad_tokens, *grads, small, rel = outs
    if ratio > 1:
        grads = [
            lax.psum_scatter(g, "dp", scatter_dimension=dim, tiled=True, axis_index_groups=groups)
            for g, dim in zip(grads, dims)
        ]
        small, rel = lax.psum((small, rel), "dp", axis_index_groups=groups)
    return (
        block_out,
        grad_tokens,
        grads[0],
        small[4:6],
        grads[1],
        small[6],
        grads[2],
        small[8:12].reshape(-1),
        grads[3],
        small[7],
        small[0],
        small[1],
        small[2],
        small[3],
        rel[:RELS, :HD],
        rel[32 : 32 + RELS, :HD],
    )


def solution(mesh):
    split = P("dp", "tensor", None)
    specs = (split, P(None, "dp", "tensor"), P(), P(("tensor", "dp"), None), P(), P("dp", "tensor"), P(),
             P(("tensor", "dp"), None))
    return jax.shard_map(
        functools.partial(on_device, mesh.shape["dp"]),
        mesh=mesh,
        in_specs=specs + (P(),) * 7 + (split,),
        out_specs=(split,) + specs + (P(),) * 7,
        check_vma=False,
    )
```

time: 809 us -> 158 us (0.20)
  waiting for transfers between devices: 389 us -> 0 us
  Pallas kernels: 0 us -> 138 us
  blocking collectives: 129 us -> 0 us
  local copies, waits for them, and re-layouts: 126 us -> 16.6 us
  matrix products: 94.7 us -> 0 us
  other arithmetic: 42.4 us -> 0 us
  between operations: 16.7 us -> 0.69 us
    reduce_scatter x11 -> x0, waiting for transfers between devices: 267 us -> none  [the longest x1 79.4 us: on_device(): lax.psum_scatter(big_total[2], 'dp', scatter_dimension=0, tiled=True)]
    pallas_call x0 -> x1, Pallas kernels: none -> 138 us  [fused_block(): pl.pallas_call(functools.partial(block_kernel, ratio, width, hid, names),...]
    dot_general x52 -> x0, matrix products: 91.6 us -> none  [the longest x2 14.1 us: on_device(): jnp.dot(forward_second_all, forward_up_w, preferred_element_type=jnp.floa...]
    all_gather x9 -> x0, blocking collectives: 86.9 us -> none  [the longest x8 62.7 us: spread(): return lax.all_gather(values, 'tensor', axis=0, tiled=True)]
    add x11 -> x0, local copies, waits for them, and re-layouts: 69.3 us -> none  [the longest x8 62 us: block_scores(): scores.reshape(head_count, grid_rows, GRID, GRID, GRID)]
    all_gather x3 -> x0, waiting for transfers between devices: 62.8 us -> none  [the longest x1 35.7 us: fetch_weights(): lax.all_gather(w_down, 'dp', axis=0, tiled=True)]
    unnamed x16 -> x0, waiting for transfers between devices: 59 us -> none
    psum x1 -> x0, blocking collectives: 42.5 us -> none  [on_device(): lax.psum((small_total[0], small_total[1], small_total[2], small_total[3],...]
  transfers between devices with their start and end apart: 15 -> 0, of which waited for: 11 -> 0; matrix products, arithmetic and copies ran while one was open for 11% -> 0% of each run, Pallas kernels for 0% -> 0%
where the time goes in v1:
time: 158 us; the launch traced here: 156 us
  Pallas kernels  138 us (87%)
  local copies, waits for them, and re-layouts  16.6 us (11%)
    pallas_call x1, Pallas kernels, fused_block(): pl.pallas_call(functools.partial(block_kernel, ratio, width, hid, names),...  138 us
    unnamed x26, local copies, waits for them, and re-layouts  6.68 us
    reshape x6, local copies, waits for them, and re-layouts, on_device(): flat = lambda v: v.reshape(1, -1)  4.17 us

profile of v1, /device:TPU:0, one launch (start us, length us, event | category | flops | bytes accessed | tf_op | source)
XLA Modules:
  0.0 155.6 jit_solution(1083701776488133472)
XLA Ops:
  0.7 1.3 reshape.56.refs_7_
  1.9 0.6 reshape.58.refs_9_
  2.5 0.1 copy-done.6
  2.6 0.6 reshape.59.refs_10_
  3.2 0.1 copy-done.7
  3.3 0.6 reshape.60.refs_11_
  3.9 0.1 copy-done.8
  4.0 0.6 reshape.61.refs_12_
  4.7 0.6 reshape.62.refs_13_
  5.3 138.4 %fused_block.1 = (bf16[2,128,768]{2,1,0:T(8,128)(2,1)}, f32[2,128,768]{2,1,0:T(8,128)}, f32[3,48,384]{2,1,0:T(8,128)}, f32[24,768]{1,0:T(8,128)}, f32[48,1536]{1...) custom-call(bf16[2,128,768]{2,1,0:T(8,128)(2,1)} %refs_0_.1, bf16[2,128,768]{2,1,0:T(8,128)(2,1)} %refs_1_.1, ...), custom_call_target="tpu_custom_call" | custom-call | tf_op jit(solution)/shard_map/fused_block/pallas_call | solution.py:734
  143.7 1.4 slice.30
  145.1 0.7 slice.32
  145.8 1.6 %slice_reduce_fusion = (f32[768]{0:T(1024)}, f32[768]{0:T(1024)}, f32[768]{0:T(1024)}, f32[768]{0:T(1024)}, f32[768]{0:T(1024)}, /*index=5*/f32[768]{0:T(1024)}) fusion(f32[16,768]{1,0:T(8,128)} %get-tuple-element.27), kind=kLoop, calls=%fused_computation | loop fusion | bytes 36864 | tf_op jit(solution)/shard_map/slice | solution.py:787
  147.4 0.6 reshape.63
  148.1 1.3 fusion
  149.4 1.8 %copy.38 = bf16[2,128,768]{2,1,0:T(8,128)(2,1)} copy(bf16[2,128,768]{2,1,0:T(8,128)(2,1)} %get-tuple-element.56) | data formatting | bytes 786432
  151.2 0.9 copy.39
  152.0 0.3 copy-done.3
  152.3 0.7 copy.40
  153.0 0.2 copy-done.4
  153.2 0.6 copy.41
  153.9 0.7 copy.42
  154.6 0.4 copy-done.1
  154.9 0.7 copy.43
  (14 shorter events, 0.1 us)
Async XLA Ops:
  0.6 1.3 copy-start.5
  1.9 0.7 copy-start.6
  2.6 0.7 copy-start.7
  3.3 0.7 copy-start.8
  4.0 0.7 copy-start.9
  143.7 7.5 %copy-start = (f32[2,128,768]{2,1,0:T(8,128)S(1)}, f32[2,128,768]{2,1,0:T(8,128)}, u32[]{:S(2)}) copy-start(f32[2,128,768]{2,1,0:T(8,128)} %get-tuple-element.57) | copy-start | bytes 2359300
  151.2 1.1 copy-start.3
  152.3 0.9 copy-start.4
  152.3 1.5 copy-start.2
  153.9 1.1 copy-start.1

commit v2 on v1

--- a/solution.py
+++ b/solution.py
@@ -125,10 +125,16 @@
         "OHF": ((TOK, PAIR), BF),
         "OHB": ((TOK, PAIR), BF),
         "MSK": ((4, 16, PAIR), BF),
-        "SMS": ((6, 16, D), F32),
-        "SMR": ((5, 16, D), F32),
-        "SRS": ((6, 64, 128), F32),
-        "SRR": ((5, 64, 128), F32),
+        "PAR": ((6, 1, D), F32),
+        "UPB": ((1, hid), F32),
+        "S0": ((4, 8, D), F32),
+        "S1": ((4, 2, D), F32),
+        "S2": ((4, 64, 128), F32),
+        "S3": ((4, 2, D), F32),
+        "R0": ((7, 8, D), F32),
+        "R1": ((7, 2, D), F32),
+        "R2": ((7, 64, 128), F32),
+        "R3": ((7, 2, D), F32),
     }
     for i, shard in enumerate(shards):
         table[f"W{i}"] = ((NZ, NX, NC) + shard, BF)
@@ -144,7 +150,7 @@
         "rsc": (4,),
         "rsx": (4, 4),
         "rsz": (4, 3),
-        "ars": (5, 2),
+        "ars": (4, 7),
     }
     return table, sems, shards
 
@@ -168,12 +174,10 @@
     def device(zz, xx, cc, tt=t):
         return (((zz * NX + xx) * NC + cc) * ratio + sub, tt)
 
-    def zrot(step):
-        return lax.rem(z + step, NZ)
-
+    z_of = (z, z + 1 - 2 * lax.rem(z, 2), lax.rem(z + 2, NZ), NZ - 1 - z)
     core_peer, x_peer, y_peer = device(z, x, 1 - c), device(z, 1 - x, c), device(z, x, c, 1 - t)
-    z_near = z + 1 - 2 * lax.rem(z, 2)
-    z_far = lax.rem(z + 2, NZ)
+    xy_peer = device(z, 1 - x, c, 1 - t)
+    z_peer = [device(zz, x, c) for zz in z_of]
     own0 = pl.multiple_of(t * half, half)
     other0 = pl.multiple_of((1 - t) * half, half)
 
@@ -195,50 +199,49 @@
     Z = [k.Z0, k.Z1, k.Z2, k.Z3]
 
     def ag_z(m, i):
-        return remote(shard_in[m], W[m].at[z, x, c], "agz", (m, i - 1), device(zrot(i), x, c))
+        return remote(shard_in[m], W[m].at[z, x, c], "agz", (m, i - 1), z_peer[i])
 
     def ag_x(m, i):
-        zz = zrot(NZ - i)
-        src = shard_in[m] if i == 0 else W[m].at[zz, x, c]
-        return remote(src, W[m].at[zz, x, c], "agx", (m, i), x_peer)
+        src = shard_in[m] if i == 0 else W[m].at[z_of[i], x, c]
+        return remote(src, W[m].at[z_of[i], x, c], "agx", (m, i), x_peer)
 
     def ag_c(m, i, other):
-        zz = zrot(NZ - i)
         xx = 1 - x if other else x
-        src = shard_in[m] if i == 0 and not other else W[m].at[zz, xx, c]
-        return remote(src, W[m].at[zz, xx, c], "agc", (m, i + 4 * other), core_peer)
-
-    def ag_start(m):
-        for i in (2, 1, 3):
+        src = shard_in[m] if i == 0 and not other else W[m].at[z_of[i], xx, c]
+        return remote(src, W[m].at[z_of[i], xx, c], "agc", (m, i + 4 * other), core_peer)
+
+    def ag_send(m, slots):
+        for i in slots:
             ag_z(m, i).start()
+
+    def ag_own(m):
         ag_x(m, 0).start()
         ag_c(m, 0, 0).start()
-        W[m][z, x, c] = shard_in[m][...]
-
-    def ag_zdone(m):
-        for i in (1, 3, 2):
+
+    def ag_pass(m, slots):
+        for i in slots:
             ag_z(m, i).wait_recv()
             ag_x(m, i).start()
             ag_c(m, i, 0).start()
 
-    def ag_xdone(m):
-        for i in (0, 1, 3, 2):
+    def ag_cross(m, slots=(0, 1, 2, 3)):
+        for i in slots:
             ag_x(m, i).wait_recv()
             ag_c(m, i, 1).start()
 
     def ag_done(m):
         for other in (0, 1):
-            for i in (0, 1, 3, 2):
+            for i in range(NZ):
                 ag_c(m, i, other).wait_recv()
 
     def rs_core(m):
         return remote(G[m].at[:, :, 1 - c], C[m], "rsc", (m,), core_peer)
 
-    def rs_x(m, zz):
-        return remote(G[m].at[zz, 1 - x, c], X[m].at[zz], "rsx", (m, zz), x_peer)
+    def rs_x(m, i):
+        return remote(G[m].at[z_of[i], 1 - x, c], X[m].at[i], "rsx", (m, i), x_peer)
 
     def rs_z(m, i):
-        return remote(G[m].at[zrot(i), x, c], Z[m].at[i - 1], "rsz", (m, i - 1), device(zrot(i), x, c))
+        return remote(G[m].at[z_of[i], x, c], Z[m].at[i - 1], "rsz", (m, i - 1), z_peer[i])
 
     def add_into(dst, where, src, which):
         if len(dst.shape) - len(where) == 3:
@@ -247,7 +250,7 @@
         else:
             dst[where] = dst[where] + src[which]
 
-    def rs_core_done(m):
+    def rs_core_done(m, starts=(2, 3, 1, 0)):
         rs_core(m).wait_recv()
 
         @pl.loop(0, NZ * NX)
@@ -255,21 +258,20 @@
             zz, xx = i // NX, lax.rem(i, NX)
             add_into(G[m], (zz, xx, c), C[m], (zz, xx))
 
-        for zz in range(NZ):
-            rs_x(m, zz).start()
-
-    def rs_x_done(m):
-        for zz in range(NZ):
-            rs_x(m, zz).wait_recv()
-
-        @pl.loop(0, NZ)
-        def _(zz):
-            add_into(G[m], (zz, x, c), X[m], (zz,))
-
-        for i in (2, 1, 3):
-            rs_z(m, i).start()
-
-    def rs_z_done(m, out):
+        rs_cross(m, starts)
+
+    def rs_cross(m, slots):
+        for i in slots:
+            rs_x(m, i).start()
+
+    def rs_pass(m, slots):
+        for i in slots:
+            rs_x(m, i).wait_recv()
+            add_into(G[m], (z_of[i], x, c), X[m], (i,))
+            if i:
+                rs_z(m, i).start()
+
+    def rs_done(m, out):
         for i in (1, 2, 3):
             rs_z(m, i).wait_recv()
         parts = range(3) if m == QKV_M else (None,)
@@ -283,6 +285,30 @@
             else:
                 out[j] = total
 
+    S = [k.S0, k.S1, k.S2, k.S3]
+    R = [k.R0, k.R1, k.R2, k.R3]
+    hops = ((0,), (1, 2, 3), (4, 5, 6))
+
+    def ar(b, i):
+        step = 0 if i == 0 else 1 if i < 4 else 2
+        peer = ([core_peer, x_peer, y_peer, xy_peer] + z_peer[1:])[i]
+        return remote(S[b].at[step], R[b].at[i], "ars", (b, i), peer)
+
+    def ar_send(step, *which):
+        for b in which:
+            for i in hops[step]:
+                ar(b, i).start()
+
+    def ar_done(step, *which):
+        for b in which:
+            for i in hops[step]:
+                ar(b, i).wait_recv()
+            if step == 0:
+                S[b][1] = S[b][0] + R[b][0]
+            else:
+                first, i = S[b][step], hops[step][0]
+                S[b][step + 1] = (first + R[b][i]) + (R[b][i + 1] + R[b][i + 2])
+
     def y_rows(img, base):
         return (img, pl.ds(base, half))
 
@@ -308,18 +334,20 @@
         return pl.ds(pl.multiple_of(base + i * CH, CH), CH)
 
     barrier = pltpu.get_barrier_semaphore()
-    peers = [core_peer, x_peer, y_peer] + [device(zrot(i), x, c) for i in (1, 2, 3)]
+    peers = [core_peer, x_peer, y_peer, xy_peer] + z_peer[1:]
     for peer in peers:
         pl.semaphore_signal(barrier, inc=1, device_id=peer, device_id_type=MESH)
     pl.semaphore_wait(barrier, len(peers))
 
-    ag_start(QKV_M)
+    ag_send(QKV_M, (1, 2))
     y_tok().start()
-    ag_start(PROJ_M)
-    ag_start(UP_M)
-    ag_start(DOWN_M)
-    y_cot().start()
-
+    for m in range(4):
+        ag_own(m)
+
+    for row, ref in enumerate((k.g1, k.b1, k.g2, k.b2, k.pjb, k.dnb)):
+        k.PAR[row] = ref[...].reshape(1, D)
+    g1, b1, g2, b2, pjb, dnb = (k.PAR.at[row] for row in range(6))
+    k.UPB[...] = k.upb[pl.ds(pl.multiple_of(t * hid, 128), hid)].reshape(1, hid)
     lane = iota((TOK, PAIR), 1)
     lane64 = lax.rem(lane, HD)
     urow, ucol = iota((TOK, PAIR), 0) // GRID, lax.rem(iota((TOK, PAIR), 0), GRID)
@@ -349,7 +377,9 @@
             bwd_tab = bwd_tab + nn(one_hot(at == td), wide)
     k.TBF[...] = fwd_tab.astype(BF)
     k.TBB[...] = bwd_tab.astype(BF)
-    k.SMS[0] = jnp.zeros((16, D), F32)
+    k.S0[0] = jnp.zeros((8, D), F32)
+    k.S1[0] = jnp.zeros((2, D), F32)
+    k.S3[0] = jnp.zeros((2, D), F32)
     k.RG[...] = jnp.zeros((PAIR, PAIR), F32)
 
     def first_norm(base):
@@ -359,17 +389,23 @@
             def _(i):
                 at = rows(base, i)
                 n, _ = normalize(k.XT[img, at].astype(F32))
-                k.FL[img, at] = (n * k.g1[...] + k.b1[...]).astype(BF)
+                k.FL[img, at] = (n * g1[...] + b1[...]).astype(BF)
 
     for img in range(IMG):
         k.XT[img, pl.ds(own0, half)] = k.tok[img]
         k.CT[img, pl.ds(own0, half)] = k.cot[img]
     first_norm(own0)
-    ag_zdone(QKV_M)
+    ag_send(QKV_M, (3,))
+    for m in range(4):
+        W[m][z, x, c] = shard_in[m][...]
+    ag_pass(QKV_M, (1, 2))
+    ag_send(PROJ_M, (1, 2, 3))
+    ag_pass(QKV_M, (3,))
+    ag_send(UP_M, (1, 2))
     y_tok().wait_recv()
+    y_cot().start()
     first_norm(other0)
-    ag_xdone(QKV_M)
-    ag_zdone(PROJ_M)
+    ag_cross(QKV_M)
     ag_done(QKV_M)
 
     lanes_w = pl.ds(pl.multiple_of(t * width, 128), width)
@@ -384,8 +420,8 @@
             for p in range(pairs):
                 k.QKV[i, p, img] = low[:, p * PAIR : (p + 1) * PAIR]
 
-    ag_zdone(UP_M)
-    ag_xdone(PROJ_M)
+    ag_pass(PROJ_M, (1, 2, 3))
+    ag_send(UP_M, (3,))
 
     def head_mask(i):
         return k.MSK[i][0:1]
@@ -426,8 +462,9 @@
     def _(step):
         attend(step)
 
-    ag_xdone(UP_M)
-    ag_zdone(DOWN_M)
+    ag_pass(UP_M, (1, 2))
+    ag_send(DOWN_M, (1, 2))
+    ag_cross(PROJ_M)
     ag_done(PROJ_M)
 
     @pl.loop(0, RING)
@@ -442,8 +479,11 @@
     def _(step):
         attend(step)
 
+    ag_pass(UP_M, (3,))
+    ag_send(DOWN_M, (3,))
     project(1)
-    ag_xdone(DOWN_M)
+    ag_pass(DOWN_M, (1, 2))
+    ag_cross(UP_M)
     ag_done(UP_M)
 
     def second(img):
@@ -456,24 +496,26 @@
                 k.XT[img, at].astype(F32)
                 + k.AP[img, at].astype(F32)
                 + k.APR[img, at].astype(F32)
-                + k.pjb[...]
+                + pjb[...]
             )
             k.MID[img, at] = mid
             n, rstd = normalize(mid)
             k.N2[img, at] = n
             k.RS2[img, at] = jnp.broadcast_to(rstd, (CH, 128))
-            k.SEC[img, at] = (n * k.g2[...] + k.b2[...]).astype(BF)
+            k.SEC[img, at] = (n * g2[...] + b2[...]).astype(BF)
 
         @pl.loop(0, hid // 256)
         def _(j):
             cols = pl.ds(pl.multiple_of(j * 256, 256), 256)
-            bias = k.upb[0:1, pl.ds(pl.multiple_of(t * hid + j * 256, 256), 256)]
+            bias = k.UPB[:, cols]
             pre = nn(k.SEC[img], W[2][:, :, :, :, cols].reshape(D, 256)) + bias
             phi = 0.5 + 0.5 * lax.erf(pre * 0.7071067811865476)
             k.ACT[img, :, cols] = (pre * phi).astype(BF)
             k.GEL[img, :, cols] = (phi + pre * (0.3989422804014327 * jnp.exp(-0.5 * pre * pre))).astype(BF)
 
     second(0)
+    ag_pass(DOWN_M, (3,))
+    ag_cross(DOWN_M)
     second(1)
     ag_done(DOWN_M)
 
@@ -482,8 +524,6 @@
         def _(j):
             cols = pl.ds(pl.multiple_of(j * 256, 256), 256)
             k.DP[img, :, cols] = nn(k.ACT[img], W[3][:, :, :, :, cols].reshape(hid, 256)).astype(BF)
-
-        y_mlp(img).start()
 
     y_cot().wait_recv()
 
@@ -499,19 +539,18 @@
 
     rs_core(DOWN_M).start()
 
-    @pl.loop(0, NZ)
-    def _(m):
-        cols = pl.ds(pl.multiple_of(m * tile, 128), tile)
-        sums = jnp.zeros((1, tile), F32)
-        for img in range(IMG):
+    per_row = D // tile
+    for img in range(IMG):
+
+        @pl.loop(0, NZ)
+        def _(m):
+            cols = pl.ds(pl.multiple_of(m * tile, 128), tile)
             grad = nt(k.CT[img], W[3][m].reshape(tile, D)) * k.GEL[img, :, cols].astype(F32)
             low = grad.astype(BF)
             k.GPRE[img, :, cols] = low
-            sums = sums + jnp.sum(low.astype(F32), axis=0, keepdims=True)
-        per_row = D // tile
-        k.SMS[0, pl.ds(8 + t * (hid // D) + m // per_row, 1), pl.ds(pl.multiple_of(lax.rem(m, per_row) * tile, 128), tile)] = sums
-
-    for img in range(IMG):
+            row = pl.ds(4 + t * (hid // D) + m // per_row, 1)
+            lanes = pl.ds(pl.multiple_of(lax.rem(m, per_row) * tile, 128), tile)
+            k.S0[0, row, lanes] = k.S0[0, row, lanes] + jnp.sum(low.astype(F32), axis=0, keepdims=True)
 
         @pl.loop(0, 2)
         def _(j):
@@ -545,7 +584,7 @@
             n = k.N2[img, at]
             rstd = jnp.concatenate([k.RS2[img, at]] * (D // 128), axis=1)
             cot = k.CT[img, at].astype(F32)
-            gm = cot + norm_back(grad, n, rstd, k.g2[...])
+            gm = cot + norm_back(grad, n, rstd, g2[...])
             k.MIDL[img, at] = gm.astype(BF)
             if own:
                 k.GM[img, rows(0, i)] = gm
@@ -555,20 +594,13 @@
 
         return lax.fori_loop(0, half // CH, chunk, (zero,) * 4 if own else ())
 
-    for img in range(IMG):
+    def middle(img):
         y_sec(img).wait_recv()
         sums = middle_back(img, own0, True)
-        for row, value in zip((2, 3, 6, 7), sums):
-            k.SMS[0, row : row + 1] = k.SMS[0, row : row + 1] + value
+        for row, value in enumerate(sums):
+            k.S0[0, row : row + 1] = k.S0[0, row : row + 1] + value
         middle_back(img, other0, False)
         k.GMX[img] = nt(k.MIDL[img], k.WPB[...]).astype(BF)
-
-    for j in range(D // 256):
-        cols = slice(j * 256, (j + 1) * 256)
-        out = tn(k.MX[...].reshape(IMG * TOK, width), k.MIDL[:, :, cols].reshape(IMG * TOK, 256))
-        G[1][:, :, :, :, cols] = out.reshape(NZ, NX, NC, width // RING, 256).astype(BF)
-    rs_core(PROJ_M).start()
-    rs_x_done(DOWN_M)
 
     def attend_back(step):
         img, p = step // pairs, lax.rem(step, pairs)
@@ -603,21 +635,41 @@
             low = grad.astype(BF)
             k.GQKV[i, img, :, cols] = low
             if i != 1:
-                row = 4 + i // 2
-                k.SMS[0, row : row + 1, lanes] = k.SMS[0, row : row + 1, lanes] + jnp.sum(
+                row = i // 2
+                k.S1[0, row : row + 1, lanes] = k.S1[0, row : row + 1, lanes] + jnp.sum(
                     low.astype(F32), axis=0, keepdims=True
                 )
+
+    middle(0)
 
     @pl.loop(0, pairs)
     def _(step):
         attend_back(step)
 
-    rs_core_done(PROJ_M)
-    rs_x_done(UP_M)
+    rs_pass(DOWN_M, (2, 3))
+    middle(1)
+    ar_send(0, 0)
+    for img in range(IMG):
+        y_mlp(img).start()
+
+    for j in range(D // 256):
+        cols = slice(j * 256, (j + 1) * 256)
+        out = tn(k.MX[...].reshape(IMG * TOK, width), k.MIDL[:, :, cols].reshape(IMG * TOK, 256))
+        G[1][:, :, :, :, cols] = out.reshape(NZ, NX, NC, width // RING, 256).astype(BF)
+    rs_core(PROJ_M).start()
+    rs_pass(DOWN_M, (1, 0))
+    ar_done(0, 0)
+    ar_send(1, 0)
 
     @pl.loop(pairs, 2 * pairs)
     def _(step):
         attend_back(step)
+
+    rg = k.RG[...]
+    turned = pltpu.roll(rg, HD, 1)
+    k.S2[0, 0:32] = rg[0:32] + turned[64:96]
+    k.S2[0, 32:64] = rg[32:64] + turned[96:128]
+    ar_send(0, 1, 2)
 
     for i in range(3):
 
@@ -628,6 +680,7 @@
             G[0][pl.ds(2 * m, 2), :, :, i] = out.reshape(2, NX, NC, D // RING, width)
 
     rs_core(QKV_M).start()
+    rs_core_done(PROJ_M)
 
     for img in range(IMG):
 
@@ -639,9 +692,20 @@
             k.GF[img, :, pl.ds(pl.multiple_of(m * (D // 2), 128), D // 2)] = total.astype(BF)
 
         y_first(img).start()
-
-    rs_core_done(QKV_M)
-    rs_x_done(PROJ_M)
+        if img == 0:
+            rs_pass(UP_M, (2, 3, 1, 0))
+            rs_core_done(QKV_M, (2, 3))
+            ar_done(0, 1, 2)
+            ar_send(1, 1, 2)
+            ar_done(1, 0)
+            ar_send(2, 0)
+
+    rs_pass(PROJ_M, (2, 3, 1, 0))
+    rs_cross(QKV_M, (1, 0))
+    rs_done(DOWN_M, k.o_gd)
+    rs_pass(QKV_M, (2, 3))
+    ar_done(1, 1, 2)
+    ar_send(2, 1, 2)
 
     for img in range(IMG):
         y_mlp(img).wait_recv()
@@ -650,54 +714,34 @@
         def finish(i, sums):
             at, here = rows(own0, i), rows(0, i)
             k.o_blk[img, here] = (
-                k.MID[img, at] + k.DP[img, at].astype(F32) + k.DPR[img, here].astype(F32) + k.dnb[...]
+                k.MID[img, at] + k.DP[img, at].astype(F32) + k.DPR[img, here].astype(F32) + dnb[...]
             ).astype(BF)
             n, rstd = normalize(k.tok[img, here].astype(F32))
             grad = k.GF[img, at].astype(F32) + k.GFR[img, here].astype(F32)
-            k.o_gtok[img, here] = k.GM[img, here] + norm_back(grad, n, rstd, k.g1[...])
+            k.o_gtok[img, here] = k.GM[img, here] + norm_back(grad, n, rstd, g1[...])
             terms = (grad * n, grad)
             return tuple(a + jnp.sum(b, axis=0, keepdims=True) for a, b in zip(sums, terms))
 
         sums = lax.fori_loop(0, half // CH, finish, (jnp.zeros((1, D), F32),) * 2)
         for row, value in enumerate(sums):
-            k.SMS[0, row : row + 1] = k.SMS[0, row : row + 1] + value
-
-    rg = k.RG[...]
-    turned = pltpu.roll(rg, HD, 1)
-    k.SRS[0, 0:32] = rg[0:32] + turned[64:96]
-    k.SRS[0, 32:64] = rg[32:64] + turned[96:128]
-
-    ar_peers = [core_peer, x_peer, y_peer, device(z_near, x, c), device(z_far, x, c)]
-
-    def ar(i):
-        return (
-            remote(k.SMS.at[i], k.SMR.at[i], "ars", (i, 0), ar_peers[i]),
-            remote(k.SRS.at[i], k.SRR.at[i], "ars", (i, 1), ar_peers[i]),
-        )
-
-    def ar_step(i):
-        for copy in ar(i):
-            copy.wait_recv()
-        k.SMS[i + 1] = k.SMS[i] + k.SMR[i]
-        k.SRS[i + 1] = k.SRS[i] + k.SRR[i]
-        if i < 4:
-            for copy in ar(i + 1):
-                copy.start()
-
-    for copy in ar(0):
-        copy.start()
-    ar_step(0)
-    rs_x_done(QKV_M)
-    rs_z_done(DOWN_M, k.o_gd)
-    ar_step(1)
-    rs_z_done(UP_M, k.o_gu)
-    ar_step(2)
-    rs_z_done(PROJ_M, k.o_gp)
-    ar_step(3)
-    ar_step(4)
-    k.o_sm[...] = k.SMS[5]
-    k.o_rel[...] = k.SRS[5]
-    rs_z_done(QKV_M, k.o_gq)
+            k.S3[0, row : row + 1] = k.S3[0, row : row + 1] + value
+
+    ar_send(0, 3)
+    rs_pass(QKV_M, (1, 0))
+    ar_done(0, 3)
+    ar_send(1, 3)
+    rs_done(UP_M, k.o_gu)
+    ar_done(2, 0)
+    ar_done(1, 3)
+    ar_send(2, 3)
+    rs_done(PROJ_M, k.o_gp)
+    ar_done(2, 1, 2)
+    k.o_sm[0:8] = k.S0[3]
+    k.o_sm[8:10] = k.S1[3]
+    k.o_rel[...] = k.S2[3]
+    ar_done(2, 3)
+    k.o_sm[10:12] = k.S3[3]
+    rs_done(QKV_M, k.o_gq)
 
     for m in range(4):
         for i in (1, 2, 3):
@@ -714,9 +758,9 @@
     for img in range(IMG):
         for make in (y_attn, y_mlp, y_sec, y_first):
             make(img).wait_send()
-    for i in range(5):
-        for copy in ar(i):
-            copy.wait_send()
+    for b in range(4):
+        for i in range(7):
+            ar(b, i).wait_send()
 
 
 def fused_block(ratio, args):
@@ -744,6 +788,47 @@
     )(*args)
 
 
+def finish_kernel(*refs):
+    big, (small, rel), outs = refs[:6], refs[6:8], refs[8:24]
+    held, sem_in, sem = refs[24:30], refs[30], refs[31]
+    where = (0, 1, 2, 4, 6, 8)
+    loads = [pltpu.make_async_copy(src, dst, sem_in.at[n]) for n, (src, dst) in enumerate(zip(big, held))]
+    copies = [pltpu.make_async_copy(src, outs[i], sem.at[n]) for n, (src, i) in enumerate(zip(held, where))]
+    for copy in loads:
+        copy.start()
+    for load, copy in zip(loads, copies):
+        load.wait()
+        copy.start()
+    outs[3][...] = small[8:10]
+    for i, row in ((5, 2), (9, 3), (10, 10), (11, 11), (12, 0), (13, 1)):
+        outs[i][...] = small[row : row + 1].reshape(D)
+    for j in range(FF // D):
+        outs[7][j * D : (j + 1) * D] = small[4 + j : 5 + j].reshape(D)
+    outs[14][...] = rel[:RELS, :HD]
+    outs[15][...] = rel[32 : 32 + RELS, :HD]
+    for copy in copies:
+        copy.wait()
+
+
+def hand_out(block_out, grad_tokens, grads, small, rel):
+    big = [block_out, grad_tokens, *grads]
+    vec = jax.ShapeDtypeStruct((D,), F32)
+    table = jax.ShapeDtypeStruct((RELS, HD), F32)
+    like = [jax.ShapeDtypeStruct(v.shape, v.dtype) for v in big]
+    outs = [like[0], like[1], like[2], jax.ShapeDtypeStruct((2, D), F32), like[3], vec, like[4],
+            jax.ShapeDtypeStruct((FF,), F32), like[5], vec, vec, vec, vec, vec, table, table]
+    vmem, whole = pl.BlockSpec(memory_space=pltpu.VMEM), pl.BlockSpec(memory_space=pl.ANY)
+    return pl.pallas_call(
+        finish_kernel,
+        out_shape=outs,
+        in_specs=[whole] * 6 + [vmem] * 2,
+        out_specs=[whole if i in (0, 1, 2, 4, 6, 8) else vmem for i in range(16)],
+        scratch_shapes=[pltpu.VMEM(v.shape, v.dtype) for v in big] + [pltpu.SemaphoreType.DMA((6,))] * 2,
+        compiler_params=pltpu.CompilerParams(vmem_limit_bytes=62 << 20),
+        name="hand_out",
+    )(*big, small, rel)
+
+
 def on_device(dp_size, *args):
     (tokens, w_qkv, qv_bias, w_proj, proj_bias, w_up, up_bias, w_down, down_bias,
      norm1_gain, norm1_shift, norm2_gain, norm2_shift, rel_rows, rel_cols, cotangent) = args
@@ -757,11 +842,10 @@
             lax.all_gather(w, "dp", axis=dim, tiled=True, axis_index_groups=groups)
             for w, dim in zip(weights, dims)
         ]
-    flat = lambda v: v.reshape(1, -1)
     outs = fused_block(
         ratio,
-        (tokens, cotangent, *weights, qv_bias, flat(proj_bias), flat(up_bias), flat(down_bias),
-         flat(norm1_gain), flat(norm1_shift), flat(norm2_gain), flat(norm2_shift), rel_rows, rel_cols),
+        (tokens, cotangent, *weights, qv_bias, proj_bias, up_bias, down_bias,
+         norm1_gain, norm1_shift, norm2_gain, norm2_shift, rel_rows, rel_cols),
     )
     block_out, grad_tokens, *grads, small, rel = outs
     if ratio > 1:
@@ -770,24 +854,7 @@
             for g, dim in zip(grads, dims)
         ]
         small, rel = lax.psum((small, rel), "dp", axis_index_groups=groups)
-    return (
-        block_out,
-        grad_tokens,
-        grads[0],
-        small[4:6],
-        grads[1],
-        small[6],
-        grads[2],
-        small[8:12].reshape(-1),
-        grads[3],
-        small[7],
-        small[0],
-        small[1],
-        small[2],
-        small[3],
-        rel[:RELS, :HD],
-        rel[32 : 32 + RELS, :HD],
-    )
+    return hand_out(block_out, grad_tokens, grads, small, rel)
 
 
 def solution(mesh):

time: 158 us -> 131 us (0.83); the launches traced: 156 us -> 131 us
  local copies, waits for them, and re-layouts: 16.6 us -> 0 us
  Pallas kernels: 138 us -> 130 us
    pallas_call x1, Pallas kernels: 138 us -> 126 us  [fused_block(): pl.pallas_call(functools.partial(block_kernel, ratio, width, hid, names),...]
    unnamed x26 -> x0, local copies, waits for them, and re-layouts: 6.68 us -> none
    slice x4 -> x0, local copies, waits for them, and re-layouts: 5.11 us -> none  [the longest x1 1.62 us: on_device(): small[3]]
    reshape x7 -> x0, local copies, waits for them, and re-layouts: 4.78 us -> none  [the longest x6 4.17 us: on_device(): flat = lambda v: v.reshape(1, -1)]
    pallas_call x0 -> x1, Pallas kernels: none -> 3.99 us  [hand_out(): pl.pallas_call(finish_kernel, out_shape=outs, in_specs=[whole] * 6 + [vme...]
where the time goes in v2:
time: 131 us
  Pallas kernels  130 us (99%)
    pallas_call x1, Pallas kernels, fused_block(): pl.pallas_call(functools.partial(block_kernel, ratio, width, hid, names),...  126 us
    pallas_call x1, Pallas kernels, hand_out(): pl.pallas_call(finish_kernel, out_shape=outs, in_specs=[whole] * 6 + [vme...  3.99 us

profile of v2, /device:TPU:0, one launch (start us, length us, event | category | flops | bytes accessed | tf_op | source)
XLA Modules:
  0.0 131.1 jit_solution(7524130127022788727)
XLA Ops:
  0.7 126.4 %fused_block.1 = (bf16[2,128,768]{2,1,0:T(8,128)(2,1)}, f32[2,128,768]{2,1,0:T(8,128)}, f32[3,48,384]{2,1,0:T(8,128)}, f32[24,768]{1,0:T(8,128)}, f32[48,1536]{1...) custom-call(bf16[2,128,768]{2,1,0:T(8,128)(2,1)} %refs_0_.1, bf16[2,128,768]{2,1,0:T(8,128)(2,1)} %refs_1_.1, ...), custom_call_target="tpu_custom_call" | custom-call | tf_op jit(solution)/shard_map/fused_block/pallas_call | solution.py:778
  127.1 4.0 %hand_out.1 = (bf16[2,128,768]{2,1,0:T(8,128)(2,1)}, f32[2,128,768]{2,1,0:T(8,128)}, f32[3,48,384]{2,1,0:T(8,128)}, f32[2,768]{1,0:T(2,128)}, f32[24,768]{1,0:T(...) custom-call(bf16[2,128,768]{2,1,0:T(8,128)(2,1)} %get-tuple-element., ...), custom_call_target="tpu_custom_call" | custom-call | tf_op jit(solution)/shard_map/hand_out/pallas_call | solution.py:821

commit v3 on v2

--- a/solution.py
+++ b/solution.py
@@ -92,16 +92,17 @@
     pairs = width // PAIR
     half = TOK // 2
     shards = [(3, D // RING, width), (width // RING, D), (D // RING, hid), (hid // RING, D)]
+    gathered = [shards[0], (2,) + shards[1], shards[2], shards[3]]
     table = {
         "XT": ((IMG, TOK, D), BF),
         "CT": ((IMG, TOK, D), BF),
-        "WPB": ((width, D), BF),
+        "WPB": ((2, width, D), BF),
+        "PSH": ((2, width // RING, D), BF),
+        "N1": ((IMG, TOK, D), BF),
         "FL": ((IMG, TOK, D), BF),
         "QKV": ((3, pairs, IMG, TOK, PAIR), BF),
         "PT": ((pairs, IMG, 2, TOK, TOK), BF),
-        "MX": ((IMG, TOK, width), BF),
-        "AP": ((IMG, TOK, D), BF),
-        "APR": ((IMG, TOK, D), BF),
+        "MX": ((2, IMG, TOK, width), BF),
         "MID": ((IMG, TOK, D), F32),
         "N2": ((IMG, TOK, D), F32),
         "RS2": ((IMG, TOK, 128), F32),
@@ -128,29 +129,28 @@
         "PAR": ((6, 1, D), F32),
         "UPB": ((1, hid), F32),
         "S0": ((4, 8, D), F32),
-        "S1": ((4, 2, D), F32),
-        "S2": ((4, 64, 128), F32),
-        "S3": ((4, 2, D), F32),
+        "S1": ((4, 4, D), F32),
+        "S2": ((4, 32, 128), F32),
         "R0": ((7, 8, D), F32),
-        "R1": ((7, 2, D), F32),
-        "R2": ((7, 64, 128), F32),
-        "R3": ((7, 2, D), F32),
+        "R1": ((7, 4, D), F32),
+        "R2": ((7, 32, 128), F32),
     }
     for i, shard in enumerate(shards):
-        table[f"W{i}"] = ((NZ, NX, NC) + shard, BF)
+        table[f"W{i}"] = ((NZ, NX, NC) + gathered[i], BF)
         table[f"G{i}"] = ((NZ, NX, NC) + shard, BF)
         table[f"C{i}"] = ((NZ, NX) + shard, BF)
         table[f"X{i}"] = ((NZ,) + shard, BF)
         table[f"Z{i}"] = ((NZ - 1,) + shard, BF)
     sems = {
         "agz": (4, 3),
+        "agh": (4, 4),
         "agx": (4, 4),
         "agc": (4, 8),
-        "ysem": (10,),
+        "ysem": (11,),
         "rsc": (4,),
         "rsx": (4, 4),
         "rsz": (4, 3),
-        "ars": (4, 7),
+        "ars": (3, 7),
     }
     return table, sems, shards
 
@@ -191,28 +191,55 @@
             device_id_type=MESH,
         )
 
-    shard_in = [k.sq, k.sp, k.su, k.sd]
+    shard_in = [k.sq, k.PSH, k.su, k.sd]
     W = [k.W0, k.W1, k.W2, k.W3]
     G = [k.G0, k.G1, k.G2, k.G3]
     C = [k.C0, k.C1, k.C2, k.C3]
     X = [k.X0, k.X1, k.X2, k.X3]
     Z = [k.Z0, k.Z1, k.Z2, k.Z3]
 
+    side = z // 2
+    relayed = (PROJ_M, UP_M, DOWN_M)
+    middle_chip = (z == 1) | (z == 2)
+    relay_of = (z, z_of[1], 2 - side, 3 - 3 * side)
+    origin = [relay_of if m in relayed else z_of for m in range(4)]
+
+    def piece(m, i, other=False):
+        if i == 0 and not other:
+            return shard_in[m]
+        return W[m].at[origin[m][i], 1 - x if other else x, c]
+
     def ag_z(m, i):
         return remote(shard_in[m], W[m].at[z, x, c], "agz", (m, i - 1), z_peer[i])
 
+    def ag_relay(m, n):
+        i, arrives, peer = ((0, 2, 3), (1, 3, 3), (2, 2, 1), (3, 3, 1))[n]
+        return pltpu.make_async_remote_copy(
+            src_ref=piece(m, i),
+            dst_ref=W[m].at[origin[m][i], x, c],
+            send_sem=k.agh_s.at[m, n],
+            recv_sem=k.agz_r.at[m, arrives - 1],
+            device_id=z_peer[peer],
+            device_id_type=MESH,
+        )
+
+    def relay(m, n):
+        @pl.when(middle_chip)
+        def _():
+            ag_relay(m, n).start()
+
     def ag_x(m, i):
-        src = shard_in[m] if i == 0 else W[m].at[z_of[i], x, c]
-        return remote(src, W[m].at[z_of[i], x, c], "agx", (m, i), x_peer)
+        return remote(piece(m, i), W[m].at[origin[m][i], x, c], "agx", (m, i), x_peer)
 
     def ag_c(m, i, other):
         xx = 1 - x if other else x
-        src = shard_in[m] if i == 0 and not other else W[m].at[z_of[i], xx, c]
-        return remote(src, W[m].at[z_of[i], xx, c], "agc", (m, i + 4 * other), core_peer)
-
-    def ag_send(m, slots):
+        return remote(piece(m, i, other), W[m].at[origin[m][i], xx, c], "agc", (m, i + 4 * other), core_peer)
+
+    def ag_send(m, slots=(1,)):
         for i in slots:
             ag_z(m, i).start()
+        if m in relayed:
+            relay(m, 0)
 
     def ag_own(m):
         ag_x(m, 0).start()
@@ -221,8 +248,27 @@
     def ag_pass(m, slots):
         for i in slots:
             ag_z(m, i).wait_recv()
+            if m in relayed:
+                relay(m, i)
             ag_x(m, i).start()
             ag_c(m, i, 0).start()
+
+    def ag_pass_middle(*pairs):
+        @pl.when(middle_chip)
+        def _():
+            for m, i in pairs:
+                ag_z(m, i).wait_recv()
+                ag_relay(m, i).start()
+                ag_x(m, i).start()
+                ag_c(m, i, 0).start()
+
+    def ag_pass_end(*pairs):
+        @pl.when(jnp.logical_not(middle_chip))
+        def _():
+            for m, i in pairs:
+                ag_z(m, i).wait_recv()
+                ag_x(m, i).start()
+                ag_c(m, i, 0).start()
 
     def ag_cross(m, slots=(0, 1, 2, 3)):
         for i in slots:
@@ -250,7 +296,7 @@
         else:
             dst[where] = dst[where] + src[which]
 
-    def rs_core_done(m, starts=(2, 3, 1, 0)):
+    def rs_core_done(m):
         rs_core(m).wait_recv()
 
         @pl.loop(0, NZ * NX)
@@ -258,15 +304,20 @@
             zz, xx = i // NX, lax.rem(i, NX)
             add_into(G[m], (zz, xx, c), C[m], (zz, xx))
 
-        rs_cross(m, starts)
-
-    def rs_cross(m, slots):
-        for i in slots:
-            rs_x(m, i).start()
-
-    def rs_pass(m, slots):
-        for i in slots:
+    queue = [(m, i) for m in (DOWN_M, UP_M, PROJ_M, QKV_M) for i in (2, 3, 1, 0)]
+    fed, taken = list(queue), list(queue)
+
+    def rs_feed(count):
+        for _ in range(count):
+            rs_x(*fed.pop(0)).start()
+
+    def rs_take(count, feed=0):
+        for _ in range(count):
+            m, i = taken.pop(0)
             rs_x(m, i).wait_recv()
+            if feed:
+                rs_feed(1)
+                feed -= 1
             add_into(G[m], (z_of[i], x, c), X[m], (i,))
             if i:
                 rs_z(m, i).start()
@@ -285,8 +336,8 @@
             else:
                 out[j] = total
 
-    S = [k.S0, k.S1, k.S2, k.S3]
-    R = [k.R0, k.R1, k.R2, k.R3]
+    S = [k.S0, k.S1, k.S2]
+    R = [k.R0, k.R1, k.R2]
     hops = ((0,), (1, 2, 3), (4, 5, 6))
 
     def ar(b, i):
@@ -319,7 +370,10 @@
         return remote(k.cot, k.CT.at[:, pl.ds(own0, half)], "ysem", (1,), y_peer)
 
     def y_attn(img):
-        return remote(k.AP.at[img], k.APR.at[img], "ysem", (2 + img,), y_peer)
+        return remote(k.MX.at[t, img], k.MX.at[t, img], "ysem", (2 + img,), y_peer)
+
+    def y_proj():
+        return remote(k.sp, k.PSH.at[t], "ysem", (10,), y_peer)
 
     def y_mlp(img):
         return remote(k.DP.at[img, pl.ds(other0, half)], k.DPR.at[img], "ysem", (4 + img,), y_peer)
@@ -340,9 +394,9 @@
     pl.semaphore_wait(barrier, len(peers))
 
     ag_send(QKV_M, (1, 2))
+    y_proj().start()
     y_tok().start()
-    for m in range(4):
-        ag_own(m)
+    ag_own(QKV_M)
 
     for row, ref in enumerate((k.g1, k.b1, k.g2, k.b2, k.pjb, k.dnb)):
         k.PAR[row] = ref[...].reshape(1, D)
@@ -378,8 +432,7 @@
     k.TBF[...] = fwd_tab.astype(BF)
     k.TBB[...] = bwd_tab.astype(BF)
     k.S0[0] = jnp.zeros((8, D), F32)
-    k.S1[0] = jnp.zeros((2, D), F32)
-    k.S3[0] = jnp.zeros((2, D), F32)
+    k.S1[0] = jnp.zeros((4, D), F32)
     k.RG[...] = jnp.zeros((PAIR, PAIR), F32)
 
     def first_norm(base):
@@ -389,22 +442,30 @@
             def _(i):
                 at = rows(base, i)
                 n, _ = normalize(k.XT[img, at].astype(F32))
+                k.N1[img, at] = n.astype(BF)
                 k.FL[img, at] = (n * g1[...] + b1[...]).astype(BF)
 
     for img in range(IMG):
         k.XT[img, pl.ds(own0, half)] = k.tok[img]
         k.CT[img, pl.ds(own0, half)] = k.cot[img]
+    k.PSH[t] = k.sp[...]
     first_norm(own0)
     ag_send(QKV_M, (3,))
+    ag_own(UP_M)
+    y_proj().wait_recv()
+    ag_own(PROJ_M)
     for m in range(4):
         W[m][z, x, c] = shard_in[m][...]
     ag_pass(QKV_M, (1, 2))
-    ag_send(PROJ_M, (1, 2, 3))
+    ag_send(UP_M)
     ag_pass(QKV_M, (3,))
-    ag_send(UP_M, (1, 2))
+    ag_send(PROJ_M)
+    ag_own(DOWN_M)
     y_tok().wait_recv()
     y_cot().start()
     first_norm(other0)
+    ag_pass(UP_M, (1,))
+    ag_pass_middle((UP_M, 2))
     ag_cross(QKV_M)
     ag_done(QKV_M)
 
@@ -420,8 +481,10 @@
             for p in range(pairs):
                 k.QKV[i, p, img] = low[:, p * PAIR : (p + 1) * PAIR]
 
-    ag_pass(PROJ_M, (1, 2, 3))
-    ag_send(UP_M, (3,))
+    ag_pass(PROJ_M, (1,))
+    ag_pass_end((UP_M, 2))
+    ag_pass_middle((PROJ_M, 2), (UP_M, 3))
+    ag_send(DOWN_M)
 
     def head_mask(i):
         return k.MSK[i][0:1]
@@ -450,54 +513,50 @@
             probs.append(low)
             vals.append(val * head_mask(head))
         mixed = tn(jnp.concatenate(probs, axis=0), jnp.concatenate(vals, axis=0))
-        k.MX[img, :, pl.ds(pl.multiple_of(p * PAIR, PAIR), PAIR)] = mixed.astype(BF)
-
-    def project(img):
-        for j in range(D // 256):
-            cols = slice(j * 256, (j + 1) * 256)
-            k.AP[img, :, cols] = nn(k.MX[img], k.WPB[:, cols]).astype(BF)
-        y_attn(img).start()
-
-    @pl.loop(0, pairs)
-    def _(step):
-        attend(step)
-
-    ag_pass(UP_M, (1, 2))
-    ag_send(DOWN_M, (1, 2))
+        k.MX[t, img, :, pl.ds(pl.multiple_of(p * PAIR, PAIR), PAIR)] = mixed.astype(BF)
+
+    attend(0)
+    attend(1)
+    ag_pass_middle((PROJ_M, 3))
+    ag_pass_end((PROJ_M, 2))
+    attend(2)
+    y_attn(0).start()
+    attend(3)
+    ag_pass(DOWN_M, (1,))
+    ag_pass_end((UP_M, 3))
+    ag_pass_middle((DOWN_M, 2))
+    attend(4)
+    ag_cross(UP_M, (0, 1))
+    attend(5)
+    y_attn(1).start()
+    ag_pass_middle((DOWN_M, 3))
+    ag_pass_end((PROJ_M, 3), (DOWN_M, 2))
+    ag_cross(UP_M, (2, 3))
     ag_cross(PROJ_M)
     ag_done(PROJ_M)
 
     @pl.loop(0, RING)
     def _(i):
         zz, xx, cc = i // (NX * NC), lax.rem(i // NC, NX), lax.rem(i, NC)
-        k.G1F[pl.ds(pl.multiple_of(i * (width // RING), 8), width // RING)] = W[1][zz, xx, cc].astype(F32)
-
-    k.WPB[...] = k.G1F[...].astype(BF)
-    project(0)
-
-    @pl.loop(pairs, 2 * pairs)
-    def _(step):
-        attend(step)
-
-    ag_pass(UP_M, (3,))
-    ag_send(DOWN_M, (3,))
-    project(1)
-    ag_pass(DOWN_M, (1, 2))
-    ag_cross(UP_M)
+        for tt in range(2):
+            at = pl.ds(pl.multiple_of(tt * width + i * (width // RING), 8), width // RING)
+            k.G1F[at] = W[1][zz, xx, cc, tt].astype(F32)
+
+    k.WPB[...] = k.G1F[...].astype(BF).reshape(2, width, D)
     ag_done(UP_M)
 
     def second(img):
         y_attn(img).wait_recv()
+
+        @pl.loop(0, D // 256)
+        def _(j):
+            cols = pl.ds(pl.multiple_of(j * 256, 256), 256)
+            k.MID[img, :, cols] = nn(k.MX[0, img], k.WPB[0, :, cols]) + nn(k.MX[1, img], k.WPB[1, :, cols])
 
         @pl.loop(0, TOK // CH)
         def _(i):
             at = rows(0, i)
-            mid = (
-                k.XT[img, at].astype(F32)
-                + k.AP[img, at].astype(F32)
-                + k.APR[img, at].astype(F32)
-                + pjb[...]
-            )
+            mid = k.MID[img, at] + k.XT[img, at].astype(F32) + pjb[...]
             k.MID[img, at] = mid
             n, rstd = normalize(mid)
             k.N2[img, at] = n
@@ -514,10 +573,10 @@
             k.GEL[img, :, cols] = (phi + pre * (0.3989422804014327 * jnp.exp(-0.5 * pre * pre))).astype(BF)
 
     second(0)
-    ag_pass(DOWN_M, (3,))
-    ag_cross(DOWN_M)
+    ag_pass_end((DOWN_M, 3))
+    ag_cross(DOWN_M, (0, 1))
     second(1)
-    ag_done(DOWN_M)
+    ag_cross(DOWN_M, (2, 3))
 
     def down(img):
         @pl.loop(0, D // 256)
@@ -540,8 +599,9 @@
     rs_core(DOWN_M).start()
 
     per_row = D // tile
-    for img in range(IMG):
-
+    ag_done(DOWN_M)
+
+    def hidden_back(img):
         @pl.loop(0, NZ)
         def _(m):
             cols = pl.ds(pl.multiple_of(m * tile, 128), tile)
@@ -559,7 +619,11 @@
 
         y_sec(img).start()
 
+    hidden_back(0)
     rs_core_done(DOWN_M)
+    rs_feed(2)
+    hidden_back(1)
+    rs_feed(1)
 
     @pl.loop(0, hid // 256)
     def _(j):
@@ -571,9 +635,12 @@
             G[2][2 * m : 2 * m + 2, :, :, :, cols] = out.reshape(2, NX, NC, D // RING, 256)
 
     rs_core(UP_M).start()
+    rs_feed(1)
     down(0)
     down(1)
     rs_core_done(UP_M)
+    rs_feed(1)
+    rs_take(2, 1)
 
     def middle_back(img, base, own):
         zero = jnp.zeros((1, D), F32)
@@ -600,7 +667,7 @@
         for row, value in enumerate(sums):
             k.S0[0, row : row + 1] = k.S0[0, row : row + 1] + value
         middle_back(img, other0, False)
-        k.GMX[img] = nt(k.MIDL[img], k.WPB[...]).astype(BF)
+        k.GMX[img] = nt(k.MIDL[img], k.WPB[t]).astype(BF)
 
     def attend_back(step):
         img, p = step // pairs, lax.rem(step, pairs)
@@ -640,24 +707,36 @@
                     low.astype(F32), axis=0, keepdims=True
                 )
 
+    def gradient_first(img):
+        @pl.loop(0, 2)
+        def _(m):
+            total = jnp.zeros((TOK, D // 2), F32)
+            for i in range(3):
+                total = total + nt(k.GQKV[i, img], W[0][pl.ds(2 * m, 2), :, :, i].reshape(D // 2, width))
+            lanes = pl.ds(pl.multiple_of(m * (D // 2), 128), D // 2)
+            k.GF[img, :, lanes] = total.astype(BF)
+            for row, value in ((2, total * k.N1[img, :, lanes].astype(F32)), (3, total)):
+                k.S1[0, row : row + 1, lanes] = k.S1[0, row : row + 1, lanes] + jnp.sum(value, axis=0, keepdims=True)
+
     middle(0)
+    rs_take(1, 1)
 
     @pl.loop(0, pairs)
     def _(step):
         attend_back(step)
 
-    rs_pass(DOWN_M, (2, 3))
+    rs_take(1, 1)
+    gradient_first(0)
     middle(1)
+    y_first(0).start()
+    y_mlp(0).start()
     ar_send(0, 0)
-    for img in range(IMG):
-        y_mlp(img).start()
 
     for j in range(D // 256):
         cols = slice(j * 256, (j + 1) * 256)
-        out = tn(k.MX[...].reshape(IMG * TOK, width), k.MIDL[:, :, cols].reshape(IMG * TOK, 256))
+        out = tn(k.MX[t].reshape(IMG * TOK, width), k.MIDL[:, :, cols].reshape(IMG * TOK, 256))
         G[1][:, :, :, :, cols] = out.reshape(NZ, NX, NC, width // RING, 256).astype(BF)
     rs_core(PROJ_M).start()
-    rs_pass(DOWN_M, (1, 0))
     ar_done(0, 0)
     ar_send(1, 0)
 
@@ -665,10 +744,14 @@
     def _(step):
         attend_back(step)
 
+    rs_core_done(PROJ_M)
+    rs_take(2, 2)
+    gradient_first(1)
+    y_first(1).start()
     rg = k.RG[...]
     turned = pltpu.roll(rg, HD, 1)
-    k.S2[0, 0:32] = rg[0:32] + turned[64:96]
-    k.S2[0, 32:64] = rg[32:64] + turned[96:128]
+    packed = pltpu.roll(rg[32:64] + turned[96:128], HD, 1)
+    k.S2[0] = jnp.where(iota((32, 128), 1) < HD, rg[0:32] + turned[64:96], packed)
     ar_send(0, 1, 2)
 
     for i in range(3):
@@ -680,72 +763,67 @@
             G[0][pl.ds(2 * m, 2), :, :, i] = out.reshape(2, NX, NC, D // RING, width)
 
     rs_core(QKV_M).start()
-    rs_core_done(PROJ_M)
-
-    for img in range(IMG):
-
-        @pl.loop(0, 2)
-        def _(m):
-            total = jnp.zeros((TOK, D // 2), F32)
-            for i in range(3):
-                total = total + nt(k.GQKV[i, img], W[0][pl.ds(2 * m, 2), :, :, i].reshape(D // 2, width))
-            k.GF[img, :, pl.ds(pl.multiple_of(m * (D // 2), 128), D // 2)] = total.astype(BF)
-
-        y_first(img).start()
-        if img == 0:
-            rs_pass(UP_M, (2, 3, 1, 0))
-            rs_core_done(QKV_M, (2, 3))
-            ar_done(0, 1, 2)
-            ar_send(1, 1, 2)
-            ar_done(1, 0)
-            ar_send(2, 0)
-
-    rs_pass(PROJ_M, (2, 3, 1, 0))
-    rs_cross(QKV_M, (1, 0))
-    rs_done(DOWN_M, k.o_gd)
-    rs_pass(QKV_M, (2, 3))
-    ar_done(1, 1, 2)
-    ar_send(2, 1, 2)
-
-    for img in range(IMG):
+    ar_done(1, 0)
+    ar_send(2, 0)
+    ar_done(0, 1, 2)
+    ar_send(1, 1, 2)
+    rs_core_done(QKV_M)
+    rs_take(2, 2)
+    rs_take(2, 2)
+
+    def finish_grad(img):
+        y_first(img).wait_recv()
+
+        @pl.loop(0, half // CH)
+        def _(i):
+            at, here = rows(own0, i), rows(0, i)
+            n, rstd = normalize(k.tok[img, here].astype(F32))
+            grad = k.GF[img, at].astype(F32) + k.GFR[img, here].astype(F32)
+            k.o_gtok[img, here] = k.GM[img, here] + norm_back(grad, n, rstd, g1[...])
+
+    def finish_block(img):
         y_mlp(img).wait_recv()
-        y_first(img).wait_recv()
-
-        def finish(i, sums):
+
+        @pl.loop(0, half // CH)
+        def _(i):
             at, here = rows(own0, i), rows(0, i)
             k.o_blk[img, here] = (
                 k.MID[img, at] + k.DP[img, at].astype(F32) + k.DPR[img, here].astype(F32) + dnb[...]
             ).astype(BF)
-            n, rstd = normalize(k.tok[img, here].astype(F32))
-            grad = k.GF[img, at].astype(F32) + k.GFR[img, here].astype(F32)
-            k.o_gtok[img, here] = k.GM[img, here] + norm_back(grad, n, rstd, g1[...])
-            terms = (grad * n, grad)
-            return tuple(a + jnp.sum(b, axis=0, keepdims=True) for a, b in zip(sums, terms))
-
-        sums = lax.fori_loop(0, half // CH, finish, (jnp.zeros((1, D), F32),) * 2)
-        for row, value in enumerate(sums):
-            k.S3[0, row : row + 1] = k.S3[0, row : row + 1] + value
-
-    ar_send(0, 3)
-    rs_pass(QKV_M, (1, 0))
-    ar_done(0, 3)
-    ar_send(1, 3)
+
+    finish_grad(0)
+    finish_block(0)
+    rs_take(1, 1)
+    finish_grad(1)
+    y_mlp(1).start()
+    ar_done(1, 1, 2)
+    ar_send(2, 1, 2)
+    rs_take(1, 1)
+    rs_done(DOWN_M, k.o_gd)
+    rs_take(1)
     rs_done(UP_M, k.o_gu)
+    rs_take(1)
     ar_done(2, 0)
-    ar_done(1, 3)
-    ar_send(2, 3)
     rs_done(PROJ_M, k.o_gp)
+    finish_block(1)
+    rs_take(1)
     ar_done(2, 1, 2)
     k.o_sm[0:8] = k.S0[3]
-    k.o_sm[8:10] = k.S1[3]
+    k.o_sm[8:12] = k.S1[3]
     k.o_rel[...] = k.S2[3]
-    ar_done(2, 3)
-    k.o_sm[10:12] = k.S3[3]
+    rs_take(1)
     rs_done(QKV_M, k.o_gq)
+
+    @pl.when(middle_chip)
+    def _():
+        for m in relayed:
+            for n in range(4):
+                ag_relay(m, n).wait_send()
 
     for m in range(4):
         for i in (1, 2, 3):
-            ag_z(m, i).wait_send()
+            if i == 1 or m not in relayed:
+                ag_z(m, i).wait_send()
             rs_z(m, i).wait_send()
         for i in range(4):
             ag_x(m, i).wait_send()
@@ -753,12 +831,12 @@
             ag_c(m, i, 1).wait_send()
             rs_x(m, i).wait_send()
         rs_core(m).wait_send()
-    for copy in (y_tok(), y_cot()):
+    for copy in (y_tok(), y_cot(), y_proj()):
         copy.wait_send()
     for img in range(IMG):
         for make in (y_attn, y_mlp, y_sec, y_first):
             make(img).wait_send()
-    for b in range(4):
+    for b in range(3):
         for i in range(7):
             ar(b, i).wait_send()
 
@@ -766,14 +844,14 @@
 def fused_block(ratio, args):
     width, hid = args[2].shape[2], args[4].shape[1]
     table, sems, shards = scratch_table(width, hid)
-    table["G1F"] = ((width, D), F32)
+    table["G1F"] = ((2 * width, D), F32)
     names = list(NAMES_IN) + list(NAMES_OUT) + list(table)
     scratch = [pltpu.VMEM(shape, kind) for shape, kind in table.values()]
     for name, shape in sems.items():
         names += [name + "_s", name + "_r"]
         scratch += [pltpu.SemaphoreType.DMA(shape)] * 2
     tok = args[0].shape
-    outs = [(tok, BF), (tok, F32)] + [(shape, F32) for shape in shards] + [((16, D), F32), ((64, 128), F32)]
+    outs = [(tok, BF), (tok, F32)] + [(shape, F32) for shape in shards] + [((16, D), F32), ((32, 128), F32)]
     vmem = pl.BlockSpec(memory_space=pltpu.VMEM)
     return pl.pallas_call(
         functools.partial(block_kernel, ratio, width, hid, names),
@@ -805,7 +883,7 @@
     for j in range(FF // D):
         outs[7][j * D : (j + 1) * D] = small[4 + j : 5 + j].reshape(D)
     outs[14][...] = rel[:RELS, :HD]
-    outs[15][...] = rel[32 : 32 + RELS, :HD]
+    outs[15][...] = rel[:RELS, HD:]
     for copy in copies:
         copy.wait()
 

time: 131 us -> 118 us (0.901)
  Pallas kernels: 130 us -> 117 us
    pallas_call x1, Pallas kernels: 126 us -> 113 us  [fused_block(): pl.pallas_call(functools.partial(block_kernel, ratio, width, hid, names),...]
where the time goes in v3:
time: 118 us
  Pallas kernels  117 us (99%)
    pallas_call x1, Pallas kernels, fused_block(): pl.pallas_call(functools.partial(block_kernel, ratio, width, hid, names),...  113 us
    pallas_call x1, Pallas kernels, hand_out(): pl.pallas_call(finish_kernel, out_shape=outs, in_specs=[whole] * 6 + [vme...  3.99 us

profile of v3, /device:TPU:0, one launch (start us, length us, event | category | flops | bytes accessed | tf_op | source)
XLA Modules:
  0.0 117.7 jit_solution(8147152514572311070)
XLA Ops:
  0.7 112.9 %fused_block.1 = (bf16[2,128,768]{2,1,0:T(8,128)(2,1)}, f32[2,128,768]{2,1,0:T(8,128)}, f32[3,48,384]{2,1,0:T(8,128)}, f32[24,768]{1,0:T(8,128)}, f32[48,1536]{1...) custom-call(bf16[2,128,768]{2,1,0:T(8,128)(2,1)} %refs_0_.1, bf16[2,128,768]{2,1,0:T(8,128)(2,1)} %refs_1_.1, ...), custom_call_target="tpu_custom_call" | custom-call | tf_op jit(solution)/shard_map/fused_block/pallas_call | solution.py:856
  113.6 4.0 %hand_out.1 = (bf16[2,128,768]{2,1,0:T(8,128)(2,1)}, f32[2,128,768]{2,1,0:T(8,128)}, f32[3,48,384]{2,1,0:T(8,128)}, f32[2,768]{1,0:T(2,128)}, f32[24,768]{1,0:T(...) custom-call(bf16[2,128,768]{2,1,0:T(8,128)(2,1)} %get-tuple-element., ...), custom_call_target="tpu_custom_call" | custom-call | tf_op jit(solution)/shard_map/hand_out/pallas_call | solution.py:899

commit v4 on v3

--- a/solution.py
+++ b/solution.py
@@ -141,15 +141,17 @@
         table[f"C{i}"] = ((NZ, NX) + shard, BF)
         table[f"X{i}"] = ((NZ,) + shard, BF)
         table[f"Z{i}"] = ((NZ - 1,) + shard, BF)
+        table[f"Y{i}"] = (shard, BF)
     sems = {
         "agz": (4, 3),
         "agh": (4, 4),
         "agx": (4, 4),
         "agc": (4, 8),
         "ysem": (11,),
-        "rsc": (4,),
+        "rsc": (4, 4),
         "rsx": (4, 4),
         "rsz": (4, 3),
+        "rsy": (4, 1),
         "ars": (3, 7),
     }
     return table, sems, shards
@@ -197,26 +199,31 @@
     C = [k.C0, k.C1, k.C2, k.C3]
     X = [k.X0, k.X1, k.X2, k.X3]
     Z = [k.Z0, k.Z1, k.Z2, k.Z3]
+    Y = [k.Y0, k.Y1, k.Y2, k.Y3]
 
     side = z // 2
     relayed = (PROJ_M, UP_M, DOWN_M)
+    broad = ()
     middle_chip = (z == 1) | (z == 2)
     relay_of = (z, z_of[1], 2 - side, 3 - 3 * side)
     origin = [relay_of if m in relayed else z_of for m in range(4)]
 
     def piece(m, i, other=False):
+        if m in broad:
+            return W[m].at[origin[m][i], :, c]
         if i == 0 and not other:
             return shard_in[m]
         return W[m].at[origin[m][i], 1 - x if other else x, c]
 
     def ag_z(m, i):
-        return remote(shard_in[m], W[m].at[z, x, c], "agz", (m, i - 1), z_peer[i])
+        dst = W[m].at[z, :, c] if m in broad else W[m].at[z, x, c]
+        return remote(piece(m, 0), dst, "agz", (m, i - 1), z_peer[i])
 
     def ag_relay(m, n):
         i, arrives, peer = ((0, 2, 3), (1, 3, 3), (2, 2, 1), (3, 3, 1))[n]
         return pltpu.make_async_remote_copy(
             src_ref=piece(m, i),
-            dst_ref=W[m].at[origin[m][i], x, c],
+            dst_ref=piece(m, i) if m in broad else W[m].at[origin[m][i], x, c],
             send_sem=k.agh_s.at[m, n],
             recv_sem=k.agz_r.at[m, arrives - 1],
             device_id=z_peer[peer],
@@ -229,13 +236,19 @@
             ag_relay(m, n).start()
 
     def ag_x(m, i):
-        return remote(piece(m, i), W[m].at[origin[m][i], x, c], "agx", (m, i), x_peer)
+        src = shard_in[m] if m in broad else piece(m, i)
+        return remote(src, W[m].at[origin[m][i], x, c], "agx", (m, i), x_peer)
 
     def ag_c(m, i, other):
+        if m in broad:
+            return remote(piece(m, i), piece(m, i), "agc", (m, i), core_peer)
         xx = 1 - x if other else x
         return remote(piece(m, i, other), W[m].at[origin[m][i], xx, c], "agc", (m, i + 4 * other), core_peer)
 
     def ag_send(m, slots=(1,)):
+        if m in broad:
+            ag_x(m, 0).wait_recv()
+            ag_c(m, 0, 0).start()
         for i in slots:
             ag_z(m, i).start()
         if m in relayed:
@@ -243,32 +256,39 @@
 
     def ag_own(m):
         ag_x(m, 0).start()
-        ag_c(m, 0, 0).start()
-
-    def ag_pass(m, slots):
+        if m not in broad:
+            ag_c(m, 0, 0).start()
+
+    def ag_on(m, i, cross=True):
+        if m not in broad and cross:
+            ag_x(m, i).start()
+        ag_c(m, i, 0).start()
+
+    def ag_pass(m, slots, cross=True):
         for i in slots:
             ag_z(m, i).wait_recv()
             if m in relayed:
                 relay(m, i)
-            ag_x(m, i).start()
-            ag_c(m, i, 0).start()
-
-    def ag_pass_middle(*pairs):
+            ag_on(m, i, cross)
+
+    def ag_pass_middle(*pairs, cross=True):
         @pl.when(middle_chip)
         def _():
             for m, i in pairs:
                 ag_z(m, i).wait_recv()
                 ag_relay(m, i).start()
-                ag_x(m, i).start()
-                ag_c(m, i, 0).start()
-
-    def ag_pass_end(*pairs):
+                ag_on(m, i, cross)
+
+    def ag_pass_end(*pairs, cross=True):
         @pl.when(jnp.logical_not(middle_chip))
         def _():
             for m, i in pairs:
                 ag_z(m, i).wait_recv()
-                ag_x(m, i).start()
-                ag_c(m, i, 0).start()
+                ag_on(m, i, cross)
+
+    def ag_late_cross(m, slots):
+        for i in slots:
+            ag_x(m, i).start()
 
     def ag_cross(m, slots=(0, 1, 2, 3)):
         for i in slots:
@@ -276,35 +296,68 @@
             ag_c(m, i, 1).start()
 
     def ag_done(m):
-        for other in (0, 1):
+        for other in (0,) if m in broad else (0, 1):
             for i in range(NZ):
                 ag_c(m, i, other).wait_recv()
 
-    def rs_core(m):
-        return remote(G[m].at[:, :, 1 - c], C[m], "rsc", (m,), core_peer)
+    def rs_core(m, i):
+        at = relay_of[i]
+        return remote(G[m].at[at, :, 1 - c], C[m].at[at], "rsc", (m, i), core_peer)
+
+    def rs_core_send(m, slots=(3, 2, 1, 0)):
+        for i in slots:
+            rs_core(m, i).start()
 
     def rs_x(m, i):
-        return remote(G[m].at[z_of[i], 1 - x, c], X[m].at[i], "rsx", (m, i), x_peer)
+        return remote(G[m].at[relay_of[i], 1 - x, c], X[m].at[i], "rsx", (m, i), x_peer)
+
+    via = jnp.where(middle_chip, 1, 2)
 
     def rs_z(m, i):
-        return remote(G[m].at[z_of[i], x, c], Z[m].at[i - 1], "rsz", (m, i - 1), z_peer[i])
+        slot = (None, 0, via, 1)[i]
+        return pltpu.make_async_remote_copy(
+            src_ref=G[m].at[relay_of[i], x, c],
+            dst_ref=Z[m].at[slot],
+            send_sem=k.rsz_s.at[m, i - 1],
+            recv_sem=k.rsz_r.at[m, slot],
+            device_id=device(relay_of[i], x, c),
+            device_id_type=MESH,
+        )
+
+    def rs_arrived(m, slot):
+        pltpu.make_async_remote_copy(
+            src_ref=Z[m].at[slot],
+            dst_ref=Z[m].at[slot],
+            send_sem=k.rsz_s.at[m, slot],
+            recv_sem=k.rsz_r.at[m, slot],
+            device_id=z_peer[1],
+            device_id_type=MESH,
+        ).wait_recv()
+
+    def rs_y(m):
+        return remote(G[m].at[relay_of[3], x, c], Y[m], "rsy", (m, 0), z_peer[1])
+
+    def rs_relay(m):
+        @pl.when(middle_chip)
+        def _():
+            rs_y(m).wait_recv()
+            add_into(G[m], (relay_of[3], x, c), Y[m], ())
+            rs_z(m, 3).start()
 
     def add_into(dst, where, src, which):
         if len(dst.shape) - len(where) == 3:
             for j in range(3):
                 dst[(*where, j)] = dst[(*where, j)] + src[(*which, j)]
         else:
-            dst[where] = dst[where] + src[which]
-
-    def rs_core_done(m):
-        rs_core(m).wait_recv()
-
-        @pl.loop(0, NZ * NX)
-        def _(i):
-            zz, xx = i // NX, lax.rem(i, NX)
-            add_into(G[m], (zz, xx, c), C[m], (zz, xx))
-
-    queue = [(m, i) for m in (DOWN_M, UP_M, PROJ_M, QKV_M) for i in (2, 3, 1, 0)]
+            dst[where] = dst[where] + src[which or ...]
+
+    def rs_core_done(m, slots=(3, 2, 1, 0)):
+        for i in slots:
+            rs_core(m, i).wait_recv()
+            for xx in range(NX):
+                add_into(G[m], (relay_of[i], xx, c), C[m], (relay_of[i], xx))
+
+    queue = [(m, i) for m in (DOWN_M, UP_M, PROJ_M, QKV_M) for i in (3, 2, 1, 0)]
     fed, taken = list(queue), list(queue)
 
     def rs_feed(count):
@@ -318,23 +371,36 @@
             if feed:
                 rs_feed(1)
                 feed -= 1
-            add_into(G[m], (z_of[i], x, c), X[m], (i,))
-            if i:
+            add_into(G[m], (relay_of[i], x, c), X[m], (i,))
+            if i == 3:
+
+                @pl.when(jnp.logical_not(middle_chip))
+                def _():
+                    rs_y(m).start()
+
+            elif i:
                 rs_z(m, i).start()
 
     def rs_done(m, out):
-        for i in (1, 2, 3):
-            rs_z(m, i).wait_recv()
+        rs_arrived(m, 0)
+        rs_arrived(m, 1)
         parts = range(3) if m == QKV_M else (None,)
-        for j in parts:
-            at = () if j is None else (j,)
-            total = G[m][(z, x, c, *at)].astype(F32)
-            for i in range(3):
-                total = total + Z[m][(i, *at)].astype(F32)
-            if j is None:
-                out[...] = total
-            else:
-                out[j] = total
+
+        def add_slots(start, slots):
+            for j in parts:
+                at = () if j is None else (j,)
+                here = ... if j is None else j
+                total = start(at, here)
+                for slot in slots:
+                    total = total + Z[m][(slot, *at)].astype(F32)
+                out[here] = total
+
+        add_slots(lambda at, here: G[m][(z, x, c, *at)].astype(F32), (0, 1))
+
+        @pl.when(middle_chip)
+        def _():
+            rs_arrived(m, 2)
+            add_slots(lambda at, here: out[here], (2,))
 
     S = [k.S0, k.S1, k.S2]
     R = [k.R0, k.R1, k.R2]
@@ -449,23 +515,23 @@
         k.XT[img, pl.ds(own0, half)] = k.tok[img]
         k.CT[img, pl.ds(own0, half)] = k.cot[img]
     k.PSH[t] = k.sp[...]
+    y_proj().wait_recv()
+    ag_own(PROJ_M)
+    ag_own(UP_M)
     first_norm(own0)
     ag_send(QKV_M, (3,))
-    ag_own(UP_M)
-    y_proj().wait_recv()
-    ag_own(PROJ_M)
     for m in range(4):
         W[m][z, x, c] = shard_in[m][...]
     ag_pass(QKV_M, (1, 2))
+    ag_send(PROJ_M)
     ag_send(UP_M)
     ag_pass(QKV_M, (3,))
-    ag_send(PROJ_M)
-    ag_own(DOWN_M)
     y_tok().wait_recv()
     y_cot().start()
     first_norm(other0)
+    ag_pass(PROJ_M, (1,))
     ag_pass(UP_M, (1,))
-    ag_pass_middle((UP_M, 2))
+    ag_pass_middle((PROJ_M, 2), (UP_M, 2))
     ag_cross(QKV_M)
     ag_done(QKV_M)
 
@@ -481,10 +547,10 @@
             for p in range(pairs):
                 k.QKV[i, p, img] = low[:, p * PAIR : (p + 1) * PAIR]
 
-    ag_pass(PROJ_M, (1,))
-    ag_pass_end((UP_M, 2))
-    ag_pass_middle((PROJ_M, 2), (UP_M, 3))
+    ag_pass_end((PROJ_M, 2), (UP_M, 2))
+    ag_pass_middle((PROJ_M, 3), (UP_M, 3))
     ag_send(DOWN_M)
+    ag_own(DOWN_M)
 
     def head_mask(i):
         return k.MSK[i][0:1]
@@ -517,22 +583,21 @@
 
     attend(0)
     attend(1)
-    ag_pass_middle((PROJ_M, 3))
-    ag_pass_end((PROJ_M, 2))
     attend(2)
     y_attn(0).start()
+    ag_pass_end((PROJ_M, 3))
+    ag_cross(PROJ_M, (0, 1))
     attend(3)
+    ag_pass_end((UP_M, 3))
     ag_pass(DOWN_M, (1,))
-    ag_pass_end((UP_M, 3))
     ag_pass_middle((DOWN_M, 2))
     attend(4)
     ag_cross(UP_M, (0, 1))
+    ag_cross(PROJ_M, (2, 3))
     attend(5)
     y_attn(1).start()
     ag_pass_middle((DOWN_M, 3))
-    ag_pass_end((PROJ_M, 3), (DOWN_M, 2))
-    ag_cross(UP_M, (2, 3))
-    ag_cross(PROJ_M)
+    ag_pass_end((DOWN_M, 2))
     ag_done(PROJ_M)
 
     @pl.loop(0, RING)
@@ -543,9 +608,8 @@
             k.G1F[at] = W[1][zz, xx, cc, tt].astype(F32)
 
     k.WPB[...] = k.G1F[...].astype(BF).reshape(2, width, D)
-    ag_done(UP_M)
-
-    def second(img):
+
+    def second_norm(img):
         y_attn(img).wait_recv()
 
         @pl.loop(0, D // 256)
@@ -563,6 +627,7 @@
             k.RS2[img, at] = jnp.broadcast_to(rstd, (CH, 128))
             k.SEC[img, at] = (n * g2[...] + b2[...]).astype(BF)
 
+    def hidden(img):
         @pl.loop(0, hid // 256)
         def _(j):
             cols = pl.ds(pl.multiple_of(j * 256, 256), 256)
@@ -572,11 +637,15 @@
             k.ACT[img, :, cols] = (pre * phi).astype(BF)
             k.GEL[img, :, cols] = (phi + pre * (0.3989422804014327 * jnp.exp(-0.5 * pre * pre))).astype(BF)
 
-    second(0)
+    second_norm(0)
+    ag_cross(UP_M, (2, 3))
+    ag_done(UP_M)
+    hidden(0)
     ag_pass_end((DOWN_M, 3))
     ag_cross(DOWN_M, (0, 1))
-    second(1)
-    ag_cross(DOWN_M, (2, 3))
+    second_norm(1)
+    hidden(1)
+    ag_cross(DOWN_M, (2,))
 
     def down(img):
         @pl.loop(0, D // 256)
@@ -588,16 +657,21 @@
 
     tile = hid // NZ
 
-    @pl.loop(0, NZ)
-    def _(m):
+    for i in (3, 2, 1, 0):
+        m = relay_of[i]
         lhs = k.ACT[:, :, pl.ds(pl.multiple_of(m * tile, 128), tile)].reshape(IMG * TOK, tile)
         for j in range(D // 256):
             cols = slice(j * 256, (j + 1) * 256)
             out = tn(lhs, k.CT[:, :, cols].reshape(IMG * TOK, 256)).astype(BF)
             G[3][m, :, :, :, cols] = out.reshape(NX, NC, hid // RING, 256)
-
-    rs_core(DOWN_M).start()
-
+        rs_core_send(DOWN_M, (i,))
+        if i == 1:
+            rs_core_done(DOWN_M, (3,))
+            rs_feed(1)
+
+    ag_cross(DOWN_M, (3,))
+    rs_core_done(DOWN_M, (2,))
+    rs_feed(1)
     per_row = D // tile
     ag_done(DOWN_M)
 
@@ -620,8 +694,8 @@
         y_sec(img).start()
 
     hidden_back(0)
-    rs_core_done(DOWN_M)
-    rs_feed(2)
+    rs_core_done(DOWN_M, (1, 0))
+    rs_feed(1)
     hidden_back(1)
     rs_feed(1)
 
@@ -634,13 +708,13 @@
             out = tn(lhs, rhs).astype(BF)
             G[2][2 * m : 2 * m + 2, :, :, :, cols] = out.reshape(2, NX, NC, D // RING, 256)
 
-    rs_core(UP_M).start()
-    rs_feed(1)
+    rs_core_send(UP_M)
+    rs_take(1)
     down(0)
+    rs_core_done(UP_M)
+    rs_feed(2)
     down(1)
-    rs_core_done(UP_M)
-    rs_feed(1)
-    rs_take(2, 1)
+    rs_take(1, 1)
 
     def middle_back(img, base, own):
         zero = jnp.zeros((1, D), F32)
@@ -720,14 +794,16 @@
 
     middle(0)
     rs_take(1, 1)
+    rs_relay(DOWN_M)
 
     @pl.loop(0, pairs)
     def _(step):
         attend_back(step)
 
-    rs_take(1, 1)
+    rs_take(1)
     gradient_first(0)
     middle(1)
+    rs_take(1)
     y_first(0).start()
     y_mlp(0).start()
     ar_send(0, 0)
@@ -736,16 +812,21 @@
         cols = slice(j * 256, (j + 1) * 256)
         out = tn(k.MX[t].reshape(IMG * TOK, width), k.MIDL[:, :, cols].reshape(IMG * TOK, 256))
         G[1][:, :, :, :, cols] = out.reshape(NZ, NX, NC, width // RING, 256).astype(BF)
-    rs_core(PROJ_M).start()
+    rs_core_send(PROJ_M)
     ar_done(0, 0)
     ar_send(1, 0)
 
-    @pl.loop(pairs, 2 * pairs)
+    attend_back(pairs)
+    rs_core_done(PROJ_M)
+    rs_feed(1)
+    rs_take(1, 1)
+    rs_relay(UP_M)
+
+    @pl.loop(pairs + 1, 2 * pairs)
     def _(step):
         attend_back(step)
 
-    rs_core_done(PROJ_M)
-    rs_take(2, 2)
+    rs_take(1, 1)
     gradient_first(1)
     y_first(1).start()
     rg = k.RG[...]
@@ -754,22 +835,22 @@
     k.S2[0] = jnp.where(iota((32, 128), 1) < HD, rg[0:32] + turned[64:96], packed)
     ar_send(0, 1, 2)
 
-    for i in range(3):
-
-        @pl.loop(0, 2)
-        def _(m):
-            lhs = k.FL[:, :, pl.ds(pl.multiple_of(m * (D // 2), 128), D // 2)].reshape(IMG * TOK, D // 2)
+    for far in (1, 0):
+        part = 1 - side if far else side
+        lhs = k.FL[:, :, pl.ds(pl.multiple_of(part * (D // 2), 128), D // 2)].reshape(IMG * TOK, D // 2)
+        for i in range(3):
             out = tn(lhs, k.GQKV[i].reshape(IMG * TOK, width)).astype(BF)
-            G[0][pl.ds(2 * m, 2), :, :, i] = out.reshape(2, NX, NC, D // RING, width)
-
-    rs_core(QKV_M).start()
+            G[0][pl.ds(2 * part, 2), :, :, i] = out.reshape(2, NX, NC, D // RING, width)
+        rs_core_send(QKV_M, (3, 2) if far else (1, 0))
+
     ar_done(1, 0)
     ar_send(2, 0)
     ar_done(0, 1, 2)
     ar_send(1, 1, 2)
+    rs_take(1, 1)
     rs_core_done(QKV_M)
-    rs_take(2, 2)
-    rs_take(2, 2)
+    rs_take(3, 3)
+    rs_relay(PROJ_M)
 
     def finish_grad(img):
         y_first(img).wait_recv()
@@ -796,13 +877,13 @@
     rs_take(1, 1)
     finish_grad(1)
     y_mlp(1).start()
+    rs_take(1)
     ar_done(1, 1, 2)
     ar_send(2, 1, 2)
-    rs_take(1, 1)
+    rs_relay(QKV_M)
     rs_done(DOWN_M, k.o_gd)
     rs_take(1)
     rs_done(UP_M, k.o_gu)
-    rs_take(1)
     ar_done(2, 0)
     rs_done(PROJ_M, k.o_gp)
     finish_block(1)
@@ -819,18 +900,28 @@
         for m in relayed:
             for n in range(4):
                 ag_relay(m, n).wait_send()
+        for m in range(4):
+            rs_z(m, 3).wait_send()
+
+    @pl.when(jnp.logical_not(middle_chip))
+    def _():
+        for m in range(4):
+            rs_y(m).wait_send()
 
     for m in range(4):
         for i in (1, 2, 3):
             if i == 1 or m not in relayed:
                 ag_z(m, i).wait_send()
-            rs_z(m, i).wait_send()
+            if i != 3:
+                rs_z(m, i).wait_send()
         for i in range(4):
-            ag_x(m, i).wait_send()
+            if i == 0 or m not in broad:
+                ag_x(m, i).wait_send()
             ag_c(m, i, 0).wait_send()
-            ag_c(m, i, 1).wait_send()
+            if m not in broad:
+                ag_c(m, i, 1).wait_send()
             rs_x(m, i).wait_send()
-        rs_core(m).wait_send()
+            rs_core(m, i).wait_send()
     for copy in (y_tok(), y_cot(), y_proj()):
         copy.wait_send()
     for img in range(IMG):

time: 118 us -> 115 us (0.975)
  Pallas kernels: 117 us -> 114 us
    pallas_call x1, Pallas kernels: 113 us -> 110 us  [fused_block(): pl.pallas_call(functools.partial(block_kernel, ratio, width, hid, names),...]
where the time goes in v4:
time: 115 us
  Pallas kernels  114 us (99%)
    pallas_call x1, Pallas kernels, fused_block(): pl.pallas_call(functools.partial(block_kernel, ratio, width, hid, names),...  110 us
    pallas_call x1, Pallas kernels, hand_out(): pl.pallas_call(finish_kernel, out_shape=outs, in_specs=[whole] * 6 + [vme...  3.99 us

profile of v4, /device:TPU:0, one launch (start us, length us, event | category | flops | bytes accessed | tf_op | source)
XLA Modules:
  0.0 114.8 jit_solution(13955765370081620801)
XLA Ops:
  0.7 110.0 %fused_block.1 = (bf16[2,128,768]{2,1,0:T(8,128)(2,1)}, f32[2,128,768]{2,1,0:T(8,128)}, f32[3,48,384]{2,1,0:T(8,128)}, f32[24,768]{1,0:T(8,128)}, f32[48,1536]{1...) custom-call(bf16[2,128,768]{2,1,0:T(8,128)(2,1)} %refs_0_.1, bf16[2,128,768]{2,1,0:T(8,128)(2,1)} %refs_1_.1, ...), custom_call_target="tpu_custom_call" | custom-call | tf_op jit(solution)/shard_map/fused_block/pallas_call | solution.py:947
  110.6 4.0 %hand_out.1 = (bf16[2,128,768]{2,1,0:T(8,128)(2,1)}, f32[2,128,768]{2,1,0:T(8,128)}, f32[3,48,384]{2,1,0:T(8,128)}, f32[2,768]{1,0:T(2,128)}, f32[24,768]{1,0:T(...) custom-call(bf16[2,128,768]{2,1,0:T(8,128)(2,1)} %get-tuple-element., ...), custom_call_target="tpu_custom_call" | custom-call | tf_op jit(solution)/shard_map/hand_out/pallas_call | solution.py:990

commit v5 on v4

--- a/solution.py
+++ b/solution.py
@@ -108,7 +108,8 @@
         "RS2": ((IMG, TOK, 128), F32),
         "SEC": ((IMG, TOK, D), BF),
         "ACT": ((IMG, TOK, hid), BF),
-        "GEL": ((IMG, TOK, hid), BF),
+        "PHI": ((IMG, TOK, hid), BF),
+        "PRE": ((IMG, TOK, hid), F32),
         "DP": ((IMG, TOK, D), BF),
         "DPR": ((IMG, half, D), BF),
         "GPRE": ((IMG, TOK, hid), BF),
@@ -295,9 +296,9 @@
             ag_x(m, i).wait_recv()
             ag_c(m, i, 1).start()
 
-    def ag_done(m):
+    def ag_done(m, pieces=range(NZ)):
         for other in (0,) if m in broad else (0, 1):
-            for i in range(NZ):
+            for i in pieces:
                 ag_c(m, i, other).wait_recv()
 
     def rs_core(m, i):
@@ -312,9 +313,10 @@
         return remote(G[m].at[relay_of[i], 1 - x, c], X[m].at[i], "rsx", (m, i), x_peer)
 
     via = jnp.where(middle_chip, 1, 2)
+    straight = (PROJ_M, QKV_M)
 
     def rs_z(m, i):
-        slot = (None, 0, via, 1)[i]
+        slot = (None, 0, via, via if m in straight else 1)[i]
         return pltpu.make_async_remote_copy(
             src_ref=G[m].at[relay_of[i], x, c],
             dst_ref=Z[m].at[slot],
@@ -372,7 +374,7 @@
                 rs_feed(1)
                 feed -= 1
             add_into(G[m], (relay_of[i], x, c), X[m], (i,))
-            if i == 3:
+            if i == 3 and m not in straight:
 
                 @pl.when(jnp.logical_not(middle_chip))
                 def _():
@@ -395,7 +397,11 @@
                     total = total + Z[m][(slot, *at)].astype(F32)
                 out[here] = total
 
-        add_slots(lambda at, here: G[m][(z, x, c, *at)].astype(F32), (0, 1))
+        own = lambda at, here: G[m][(z, x, c, *at)].astype(F32)
+        if m in straight:
+            rs_arrived(m, 2)
+            return add_slots(own, (0, 1, 2))
+        add_slots(own, (0, 1))
 
         @pl.when(middle_chip)
         def _():
@@ -581,6 +587,17 @@
         mixed = tn(jnp.concatenate(probs, axis=0), jnp.concatenate(vals, axis=0))
         k.MX[t, img, :, pl.ds(pl.multiple_of(p * PAIR, PAIR), PAIR)] = mixed.astype(BF)
 
+    part, each = width // NZ, width // RING
+
+    def proj_ready(pieces):
+        ag_done(PROJ_M, pieces)
+        for i in pieces:
+            zz = relay_of[i]
+            for tt in range(2):
+                for n in range(NX * NC):
+                    k.G1F[n * each : (n + 1) * each] = W[1][zz, n // NC, n % NC, tt].astype(F32)
+                k.WPB[tt, pl.ds(pl.multiple_of(zz * part, 16), part)] = k.G1F[...].astype(BF)
+
     attend(0)
     attend(1)
     attend(2)
@@ -594,20 +611,12 @@
     attend(4)
     ag_cross(UP_M, (0, 1))
     ag_cross(PROJ_M, (2, 3))
+    proj_ready((0, 1))
     attend(5)
     y_attn(1).start()
     ag_pass_middle((DOWN_M, 3))
     ag_pass_end((DOWN_M, 2))
-    ag_done(PROJ_M)
-
-    @pl.loop(0, RING)
-    def _(i):
-        zz, xx, cc = i // (NX * NC), lax.rem(i // NC, NX), lax.rem(i, NC)
-        for tt in range(2):
-            at = pl.ds(pl.multiple_of(tt * width + i * (width // RING), 8), width // RING)
-            k.G1F[at] = W[1][zz, xx, cc, tt].astype(F32)
-
-    k.WPB[...] = k.G1F[...].astype(BF).reshape(2, width, D)
+    proj_ready((2, 3))
 
     def second_norm(img):
         y_attn(img).wait_recv()
@@ -635,7 +644,8 @@
             pre = nn(k.SEC[img], W[2][:, :, :, :, cols].reshape(D, 256)) + bias
             phi = 0.5 + 0.5 * lax.erf(pre * 0.7071067811865476)
             k.ACT[img, :, cols] = (pre * phi).astype(BF)
-            k.GEL[img, :, cols] = (phi + pre * (0.3989422804014327 * jnp.exp(-0.5 * pre * pre))).astype(BF)
+            k.PRE[img, :, cols] = pre
+            k.PHI[img, :, cols] = phi.astype(BF)
 
     second_norm(0)
     ag_cross(UP_M, (2, 3))
@@ -679,7 +689,9 @@
         @pl.loop(0, NZ)
         def _(m):
             cols = pl.ds(pl.multiple_of(m * tile, 128), tile)
-            grad = nt(k.CT[img], W[3][m].reshape(tile, D)) * k.GEL[img, :, cols].astype(F32)
+            pre = k.PRE[img, :, cols]
+            slope = k.PHI[img, :, cols].astype(F32) + pre * (0.3989422804014327 * jnp.exp(-0.5 * pre * pre))
+            grad = nt(k.CT[img], W[3][m].reshape(tile, D)) * slope
             low = grad.astype(BF)
             k.GPRE[img, :, cols] = low
             row = pl.ds(4 + t * (hid // D) + m // per_row, 1)
@@ -850,7 +862,6 @@
     rs_take(1, 1)
     rs_core_done(QKV_M)
     rs_take(3, 3)
-    rs_relay(PROJ_M)
 
     def finish_grad(img):
         y_first(img).wait_recv()
@@ -873,14 +884,13 @@
             ).astype(BF)
 
     finish_grad(0)
+    rs_take(1, 1)
+    rs_take(1)
     finish_block(0)
-    rs_take(1, 1)
     finish_grad(1)
     y_mlp(1).start()
-    rs_take(1)
     ar_done(1, 1, 2)
     ar_send(2, 1, 2)
-    rs_relay(QKV_M)
     rs_done(DOWN_M, k.o_gd)
     rs_take(1)
     rs_done(UP_M, k.o_gu)
@@ -901,18 +911,20 @@
             for n in range(4):
                 ag_relay(m, n).wait_send()
         for m in range(4):
-            rs_z(m, 3).wait_send()
+            if m not in straight:
+                rs_z(m, 3).wait_send()
 
     @pl.when(jnp.logical_not(middle_chip))
     def _():
         for m in range(4):
-            rs_y(m).wait_send()
+            if m not in straight:
+                rs_y(m).wait_send()
 
     for m in range(4):
         for i in (1, 2, 3):
             if i == 1 or m not in relayed:
                 ag_z(m, i).wait_send()
-            if i != 3:
+            if i != 3 or m in straight:
                 rs_z(m, i).wait_send()
         for i in range(4):
             if i == 0 or m not in broad:
@@ -935,7 +947,7 @@
 def fused_block(ratio, args):
     width, hid = args[2].shape[2], args[4].shape[1]
     table, sems, shards = scratch_table(width, hid)
-    table["G1F"] = ((2 * width, D), F32)
+    table["G1F"] = ((width // NZ, D), F32)
     names = list(NAMES_IN) + list(NAMES_OUT) + list(table)
     scratch = [pltpu.VMEM(shape, kind) for shape, kind in table.values()]
     for name, shape in sems.items():

time: 115 us -> 114 us (level)
    pallas_call x1, Pallas kernels: 110 us -> 109 us  [fused_block(): pl.pallas_call(functools.partial(block_kernel, ratio, width, hid, names),...]
where the time goes in v5:
time: 114 us
  Pallas kernels  113 us (99%)
    pallas_call x1, Pallas kernels, fused_block(): pl.pallas_call(functools.partial(block_kernel, ratio, width, hid, names),...  109 us
    pallas_call x1, Pallas kernels, hand_out(): pl.pallas_call(finish_kernel, out_shape=outs, in_specs=[whole] * 6 + [vme...  3.99 us

profile of v5, /device:TPU:0, one launch (start us, length us, event | category | flops | bytes accessed | tf_op | source)
XLA Modules:
  0.0 113.6 jit_solution(10717393263038627970)
XLA Ops:
  0.7 108.8 %fused_block.1 = (bf16[2,128,768]{2,1,0:T(8,128)(2,1)}, f32[2,128,768]{2,1,0:T(8,128)}, f32[3,48,384]{2,1,0:T(8,128)}, f32[24,768]{1,0:T(8,128)}, f32[48,1536]{1...) custom-call(bf16[2,128,768]{2,1,0:T(8,128)(2,1)} %refs_0_.1, bf16[2,128,768]{2,1,0:T(8,128)(2,1)} %refs_1_.1, ...), custom_call_target="tpu_custom_call" | custom-call | tf_op jit(solution)/shard_map/fused_block/pallas_call | solution.py:959
  109.4 4.0 %hand_out.1 = (bf16[2,128,768]{2,1,0:T(8,128)(2,1)}, f32[2,128,768]{2,1,0:T(8,128)}, f32[3,48,384]{2,1,0:T(8,128)}, f32[2,768]{1,0:T(2,128)}, f32[24,768]{1,0:T(...) custom-call(bf16[2,128,768]{2,1,0:T(8,128)(2,1)} %get-tuple-element., ...), custom_call_target="tpu_custom_call" | custom-call | tf_op jit(solution)/shard_map/hand_out/pallas_call | solution.py:1002

commit v6 on v5

--- a/solution.py
+++ b/solution.py
@@ -83,7 +83,7 @@
     "g2", "b2", "relr", "relc",
 )
 NAMES_OUT = (
-    "o_blk", "o_gtok", "o_gq", "o_gp", "o_gu", "o_gd",
+    "h_blk", "h_gtok", "o_gq", "h_gp", "h_gu", "h_gd",
     "o_sm", "o_rel",
 )
 
@@ -153,6 +153,7 @@
         "rsx": (4, 4),
         "rsz": (4, 3),
         "rsy": (4, 1),
+        "outs": (5,),
         "ars": (3, 7),
     }
     return table, sems, shards
@@ -458,6 +459,10 @@
 
     def rows(base, i):
         return pl.ds(pl.multiple_of(base + i * CH, CH), CH)
+
+    def hand_over(n):
+        src, dst = ((k.o_gd, k.h_gd), (k.o_gu, k.h_gu), (k.o_gp, k.h_gp), (k.o_gtok, k.h_gtok), (k.o_blk, k.h_blk))[n]
+        return pltpu.make_async_copy(src, dst, k.outs_s.at[n])
 
     barrier = pltpu.get_barrier_semaphore()
     peers = [core_peer, x_peer, y_peer, xy_peer] + z_peer[1:]
@@ -891,12 +896,17 @@
     y_mlp(1).start()
     ar_done(1, 1, 2)
     ar_send(2, 1, 2)
+    hand_over(3).start()
     rs_done(DOWN_M, k.o_gd)
+    hand_over(0).start()
     rs_take(1)
     rs_done(UP_M, k.o_gu)
+    hand_over(1).start()
     ar_done(2, 0)
     rs_done(PROJ_M, k.o_gp)
+    hand_over(2).start()
     finish_block(1)
+    hand_over(4).start()
     rs_take(1)
     ar_done(2, 1, 2)
     k.o_sm[0:8] = k.S0[3]
@@ -904,6 +914,9 @@
     k.o_rel[...] = k.S2[3]
     rs_take(1)
     rs_done(QKV_M, k.o_gq)
+
+    for n in range(5):
+        hand_over(n).wait()
 
     @pl.when(middle_chip)
     def _():
@@ -955,12 +968,16 @@
         scratch += [pltpu.SemaphoreType.DMA(shape)] * 2
     tok = args[0].shape
     outs = [(tok, BF), (tok, F32)] + [(shape, F32) for shape in shards] + [((16, D), F32), ((32, 128), F32)]
+    for name, (shape, kind) in zip(("o_blk", "o_gtok", "o_gp", "o_gu", "o_gd"), (outs[0], outs[1], outs[3], outs[4], outs[5])):
+        names.append(name)
+        scratch.append(pltpu.VMEM(shape, kind))
     vmem = pl.BlockSpec(memory_space=pltpu.VMEM)
+    whole = pl.BlockSpec(memory_space=pl.ANY)
     return pl.pallas_call(
         functools.partial(block_kernel, ratio, width, hid, names),
         out_shape=[jax.ShapeDtypeStruct(shape, kind) for shape, kind in outs],
         in_specs=[vmem] * len(NAMES_IN),
-        out_specs=[vmem] * len(outs),
+        out_specs=[whole, whole, vmem, whole, whole, whole, vmem, vmem],
         scratch_shapes=scratch,
         compiler_params=pltpu.CompilerParams(
             collective_id=0, has_side_effects=True, vmem_limit_bytes=62 << 20

time: 114 us -> 113 us (level)
  no operation moved by 1% of the time
where the time goes in v6:
time: 113 us
  Pallas kernels  112 us (99%)
    pallas_call x1, Pallas kernels, fused_block(): pl.pallas_call(functools.partial(block_kernel, ratio, width, hid, names),...  108 us
    pallas_call x1, Pallas kernels, hand_out(): pl.pallas_call(finish_kernel, out_shape=outs, in_specs=[whole] * 6 + [vme...  3.99 us

profile of v6, /device:TPU:0, one launch (start us, length us, event | category | flops | bytes accessed | tf_op | source)
XLA Modules:
  0.0 113.1 jit_solution(14257433429861548256)
XLA Ops:
  0.7 108.3 %fused_block.1 = (bf16[2,128,768]{2,1,0:T(8,128)(2,1)}, f32[2,128,768]{2,1,0:T(8,128)}, f32[3,48,384]{2,1,0:T(8,128)}, f32[24,768]{1,0:T(8,128)}, f32[48,1536]{1...) custom-call(bf16[2,128,768]{2,1,0:T(8,128)(2,1)} %refs_0_.1, bf16[2,128,768]{2,1,0:T(8,128)(2,1)} %refs_1_.1, ...), custom_call_target="tpu_custom_call" | custom-call | tf_op jit(solution)/shard_map/fused_block/pallas_call | solution.py:976
  108.9 4.0 %hand_out.1 = (bf16[2,128,768]{2,1,0:T(8,128)(2,1)}, f32[2,128,768]{2,1,0:T(8,128)}, f32[3,48,384]{2,1,0:T(8,128)}, f32[2,768]{1,0:T(2,128)}, f32[24,768]{1,0:T(...) custom-call(bf16[2,128,768]{2,1,0:T(8,128)(2,1)} %get-tuple-element., ...), custom_call_target="tpu_custom_call" | custom-call | tf_op jit(solution)/shard_map/hand_out/pallas_call | solution.py:1019
